TPU v7x, 512 devices: a whole 4x4x16 slice. The times are simulated.
512 devices in a mesh: pat: 32 (over x, z_lo), ori: 16 (over z_hi, y, core).
Axes of the slice: x: 4, y: 4, z: 16 (z_hi: 2, z_lo: 8; z = z_hi * 8 + z_lo), core: 2. Of those that a mesh axis runs over, the one named last changes fastest.
Arguments:
- patterns: bfloat16 [12288, 4096], P('pat'), may hold values from 0 to 240, as said below
- mask: int32 [12288], P('pat'), may hold values 0 or 1
- model: float32 [1024, 64], replicated, may hold values from -0.09375 to 0.09375
- wigner: bfloat16 [2048, 1024], P('ori'), may hold values from -6 to 6
Outputs:
- harmonics: float32 [1024, 64], P('ori', 'pat')
Inputs may be any that keep to these rules, and one draw needn't show every extreme that they name: `patterns`: photon counts scaled by each pattern's fluence and each pixel's response.
All inputs are finite; a program needn't handle non-finite values. No bound on the sum of `mask` on one device may be relied on, other than what follows from the above.
Results may differ from a plain program's by a relative error of at most 0.0075.
Values may be sent and summed in bfloat16 or wider, within the bound.
A program may use at most 64 MiB of HBM per device.

v0:
```python
import math

import jax
import jax.numpy as jnp
from jax import lax
from jax.sharding import PartitionSpec as P

RADII = 64
ANGLES = 64
DEG = 16
ORD = 64
PIX = 4096


temper = 0.05
background = 0.1


def order_table():
    orders = jnp.arange(ORD, dtype=jnp.int32)[:, None]
    angles = jnp.arange(ANGLES, dtype=jnp.int32)[None, :]
    half_way = ANGLES // 2
    phase_cos = 2.0 * math.pi / ANGLES * (orders * angles).astype(jnp.float32)
    phase_sin = 2.0 * math.pi / ANGLES * ((orders - half_way) * angles).astype(jnp.float32)
    return jnp.where(orders <= half_way, jnp.cos(phase_cos), jnp.sin(phase_sin))


def local(patterns, mask, model, wigner):
    highest = lax.Precision.HIGHEST
    contract_first = (((0,), (0,)), ((), ()))
    pat_count = lax.axis_size("pat")
    ori_count = lax.axis_size("ori")
    own_orients = wigner.shape[0]
    orients = own_orients * ori_count
    inv_root = 1.0 / math.sqrt(orients)
    synthesis = order_table()
    forward = synthesis * (2.0 / ANGLES)
    rows_own = wigner.astype(jnp.float32).reshape(own_orients, ORD, DEG)
    cycle_model = jnp.einsum(
        "rkd,kdb->kbr", rows_own, model.reshape(ORD, DEG, RADII), precision=highest
    )
    log_slices = (
        (background + jnp.einsum("kbr,ka->bar", cycle_model, synthesis, precision=highest))
        .reshape(PIX, own_orients)
        .astype(jnp.bfloat16)
    )
    intensity = jnp.sum(jnp.exp(log_slices.astype(jnp.float32)), axis=0)
    products = jnp.dot(patterns, log_slices, preferred_element_type=jnp.float32)
    scores = temper * (products - intensity[None, :])
    local_peak = jnp.max(scores, axis=1)
    row_peak = lax.pmax(local_peak, "ori")
    exponent = jnp.exp(scores - row_peak[:, None])
    row_mass = lax.psum(jnp.sum(exponent, axis=1), "ori")
    factor = 1.0 / row_mass
    weights = (exponent * (factor * mask.astype(jnp.float32))[:, None]).astype(jnp.bfloat16)
    occupancy = lax.psum(jnp.sum(weights.astype(jnp.float32), axis=0), "pat")
    pix_share = PIX // pat_count
    cycle_count = pix_share // ANGLES
    order_share = ORD // ori_count
    order_columns = lax.all_to_all(wigner, "ori", split_axis=1, concat_axis=0, tiled=True)
    rows_orders = order_columns.astype(jnp.float32).reshape(orients, order_share, DEG)
    weighted = lax.psum_scatter(
        lax.dot_general(
            patterns, weights, contract_first, preferred_element_type=jnp.float32
        ).astype(jnp.bfloat16),
        "pat",
        scatter_dimension=0,
        tiled=True,
    ).astype(jnp.float32)
    slices = weighted / (occupancy + 1.0)[None, :]
    cycle_data = jnp.einsum(
        "ka,bar->kbr", forward, slices.reshape(cycle_count, ANGLES, own_orients), precision=highest
    )
    gathered = (
        jnp.einsum(
            "rkd,kbr->kdb",
            rows_orders,
            lax.all_to_all(cycle_data, "ori", split_axis=0, concat_axis=2, tiled=True),
            precision=highest,
        )
        * inv_root
    )
    return gathered.reshape(order_share * DEG, cycle_count)


def solution(mesh):
    return jax.shard_map(
        local,
        mesh=mesh,
        in_specs=(P("pat", None), P("pat"), P(), P("ori", None)),
        out_specs=P("ori", "pat"),
        check_vma=False,
    )
```

profile of v0, /device:TPU:1, one launch (start us, length us, event | category | flops | bytes accessed | tf_op | source)
XLA Modules:
  0.0 432.9 jit_solution(17902879810815251091)
XLA Ops:
  6.5 0.0 copy-start
  6.5 0.0 reduce-scatter.4.cloned.1.call-start
  6.6 1.3 copy.19
  7.8 0.0 copy-start.1
  7.8 2.0 copy.18
  9.9 2.9 fusion.32
  12.8 3.7 exponential_reduce_fusion
  16.4 0.0 copy-done.1
  16.4 0.0 copy-done
  16.4 0.0 copy-start.2
  16.4 1.1 fusion.31
  17.6 68.2 %pmax.7 = f32[384]{0:T(512)S(1)} all-reduce(f32[384]{0:T(512)S(1)} %get-tuple-element.7), channel_id=1, replica_groups=mesh['pat'=32,'ori'=16] {'ori'}, use_global_device_ids=true, to_apply=%region_2.3 | all-reduce | flops 384 | bytes 3072 | tf_op jit(solution)/shard_map/pmax | solution.py:51
  85.7 0.1 fusion.7
  85.8 72.4 %psum.14 = f32[384]{0:T(512)S(1)} all-reduce(f32[384]{0:T(512)S(1)} %fusion.7), channel_id=1, replica_groups=mesh['pat'=32,'ori'=16] {'ori'}, use_global_device_ids=true, to_apply=%region_4.5 | all-reduce | flops 384 | bytes 3072 | tf_op jit(solution)/shard_map/psum | solution.py:53
  158.2 0.0 copy-done.2
  158.2 1.8 fusion
  160.0 2.3 copy.30
  162.3 0.0 reduce-scatter.4.cloned.1.call-update
  162.3 4.6 %all-to-all-start.1 = ((bf16[128,16,64]{0,2,1:T(8,128)(2,1)}), bf16[128,16,64]{0,2,1:T(8,128)(2,1)}, u32[]{:S(2)}, u32[]{:S(2)}) async-start(bf16[128,16,64]{0,2,1:T(8,128)(2,1)} %bitcast.41), calls=%async_computation.1 | async-start | bytes 524288 | tf_op jit(solution)/shard_map/all_to_all | solution.py:60
  166.9 0.1 convert_reduce_fusion
  167.0 108.6 %psum.15 = f32[128]{0:T(128)S(1)} all-reduce(f32[128]{0:T(128)S(1)} %convert_reduce_fusion), channel_id=1, replica_groups=mesh['pat'=32,'ori'=16] {'pat'}, use_global_device_ids=true, to_apply=%region_7.8 | all-reduce | flops 128 | bytes 1024 | tf_op jit(solution)/shard_map/psum | solution.py:56
  275.6 101.2 %reduce-scatter.4.cloned.1.call-done = bf16[128,128]{1,0:T(8,128)(2,1)} async-done(((bf16[4096,128]{1,0:T(8,128)(2,1)}), bf16[128,128]{1,0:T(8,128)(2,1)}) %reduce-scatter.4.cloned.1.call-update) | async-done | bytes 32784 | tf_op jit(solution)/shard_map/reduce_scatter | solution.py:62
  376.8 0.8 convert_divide_fusion
  377.5 0.5 fusion.16
  378.0 0.7 copy.23
  378.7 0.0 all-to-all-done.1
  378.7 30.7 %all-to-all-start = ((f32[64,2,128]{2,1,0:T(2,128)}), f32[64,2,128]{2,1,0:T(2,128)S(1)}, u32[]{:S(2)}, u32[]{:S(2)}) async-start(f32[64,2,128]{2,1,0:T(2,128)} %copy.23), calls=%async_computation | async-start | bytes 131072 | tf_op jit(solution)/shard_map/all_to_all | solution.py:78
  409.4 1.1 copy.26
  410.5 0.8 reshape.38
  411.3 12.6 %all-to-all-done = f32[64,2,128]{2,1,0:T(2,128)S(1)} async-done(((f32[64,2,128]{2,1,0:T(2,128)}), f32[64,2,128]{2,1,0:T(2,128)S(1)}, u32[]{:S(2)}, u32[]{:S(2)}) %all-to-all-start) | async-done | bytes 65568 | tf_op jit(solution)/shard_map/all_to_all | solution.py:78
  424.0 1.3 fusion.6
  425.4 0.7 reshape.39
  (7 shorter events, 0.1 us)
Async XLA Ops:
  6.5 9.9 %copy-start = (bf16[384,4096]{1,0:T(8,128)(2,1)S(1)}, bf16[384,4096]{1,0:T(8,128)(2,1)}, u32[]{:S(2)}) copy-start(bf16[384,4096]{1,0:T(8,128)(2,1)} %param.4) | copy-start | bytes 9437188
  6.5 370.2 %reduce-scatter.4.cloned.1.call-start = ((), (), s32[]{:S(2)}) async-start(), calls=%async_computation.3 | async-start | bytes 1081344 | tf_op jit(solution)/shard_map/reduce_scatter | solution.py:62
  7.8 8.6 %copy-start.1 = (bf16[128,1024]{0,1:T(8,128)(2,1)}, bf16[128,1024]{0,1:T(8,128)(2,1)S(1)}, u32[]{:S(2)}) copy-start(bf16[128,1024]{0,1:T(8,128)(2,1)S(1)} %copy.19) | copy-start | bytes 786436
  16.4 141.8 %copy-start.2 = (s32[384]{0:T(512)S(1)}, s32[384]{0:T(512)}, u32[]{:S(2)}) copy-start(s32[384]{0:T(512)} %param.5) | copy-start | bytes 4612
  162.3 216.4 %all-to-all-start.1 = ((bf16[128,16,64]{0,2,1:T(8,128)(2,1)}), bf16[128,16,64]{0,2,1:T(8,128)(2,1)}, u32[]{:S(2)}, u32[]{:S(2)}) async-start(bf16[128,16,64]{0,2,1:T(8,128)(2,1)} %bitcast.41), calls=%async_computation.1 | async-start | bytes 524288 | tf_op jit(solution)/shard_map/all_to_all | solution.py:60
  378.7 45.2 %all-to-all-start = ((f32[64,2,128]{2,1,0:T(2,128)}), f32[64,2,128]{2,1,0:T(2,128)S(1)}, u32[]{:S(2)}, u32[]{:S(2)}) async-start(f32[64,2,128]{2,1,0:T(2,128)} %copy.23), calls=%async_computation | async-start | bytes 131072 | tf_op jit(solution)/shard_map/all_to_all | solution.py:78
Sparse Core Ops, SparseCore 0:
  162.4 214.3 reduce-scatter.3
where the time goes:
time: 433 us
  blocking collectives  249 us (58%)
  waiting for transfers between devices  114 us (26%)
  starting transfers between devices  35.3 us (8%)
  between operations  13.5 us (3%)
  matrix products  11.2 us (3%)
  local copies, waits for them, and re-layouts  8.91 us (2%)
    psum x1, blocking collectives, local(): occupancy = lax.psum(jnp.sum(weights.astype(jnp.float32), axis=0), 'pat')  109 us
    reduce_scatter x1, waiting for transfers between devices, local(): lax.psum_scatter(lax.dot_general(patterns, weights, contract_first, prefe...  101 us
    psum x1, blocking collectives, local(): row_mass = lax.psum(jnp.sum(exponent, axis=1), 'ori')  72.4 us
    pmax x1, blocking collectives, local(): row_peak = lax.pmax(local_peak, 'ori')  68.2 us
    all_to_all x1, starting transfers between devices, local(): lax.all_to_all(cycle_data, 'ori', split_axis=0, concat_axis=2, tiled=True)  30.7 us
    all_to_all x1, waiting for transfers between devices, local(): lax.all_to_all(cycle_data, 'ori', split_axis=0, concat_axis=2, tiled=True)  12.6 us
  transfers between devices with their start and end apart: 3, of which 2 were waited for; matrix products, arithmetic and copies ran while one was open for 1% of the time, Pallas kernels for 0%

commit v1 on v0

v1 whole, which is shorter than its diff:
```python
import math

import jax
import jax.numpy as jnp
import numpy as np
from jax import lax
from jax.experimental import pallas as pl
from jax.experimental.pallas import tpu as pltpu
from jax.sharding import PartitionSpec as P

RADII = 64
ANGLES = 64
DEG = 16
ORD = 64
PIX = 4096
HARM = 1024
PATTERNS = 12288
ORIENTS = 2048

TEMPER = 0.05
BACKGROUND = 0.1

NX, NZ = 4, 8
NH, NQ = 2, 8
PLANE = NX * NQ
RING = NH * NZ
OWN_P = PATTERNS // (NX * NZ)
OWN_R = ORIENTS // (NH * NQ)
PT = OWN_P // 128
BLK = 4 * ANGLES
NBLK = PIX // BLK

F32 = jnp.float32
BF16 = jnp.bfloat16
MESH = pl.DeviceIdType.MESH


def order_table():
    orders = np.arange(ORD)[:, None]
    angles = np.arange(ANGLES)[None, :]
    half = ANGLES // 2
    step = 2.0 * math.pi / ANGLES
    cos = np.cos(step * ((orders * angles) % ANGLES))
    sin = np.sin(step * (((orders - half) * angles) % ANGLES))
    return np.where(orders <= half, cos, sin).astype(np.float32)


def two_terms(block):
    full = np.kron(np.eye(4, dtype=np.float32), block.astype(np.float32))
    high = full.astype(BF16)
    low = (full - high.astype(np.float32)).astype(BF16)
    return np.stack([high, low])


def split(value):
    high = value.astype(BF16)
    low = (value - high.astype(F32)).astype(BF16)
    return high, low


def dot(a, b):
    return jnp.dot(a, b, preferred_element_type=F32)


def apply_table(table_ref, value):
    high, low = split(value)
    both = dot(table_ref[0], jnp.concatenate([high, low], axis=1))
    return both[:, :OWN_R] + both[:, OWN_R:] + dot(table_ref[1], high)


def kernel(
    pat_hbm, mask_ref, model_ref, wig_ref, syn_ref, fwd_ref, out_ref,
    pat, pat_t, cyc, logs, score, wig_p, wt, ordt,
    stat, b1, pair, b2, occ1, c1, occ2, c2, harm, e1, zsum, zsend, e2,
    in_sem, b1_s, b1_r, b2_s, b2_r, c1_s, c1_r, c2_s, c2_r, e1_s, e1_r, e2_s, e2_r,
):
    p_id = lax.axis_index("pat")
    o_id = lax.axis_index("ori")
    x, zl = lax.div(p_id, NZ), lax.rem(p_id, NZ)
    zh, q = lax.div(o_id, NQ), lax.rem(o_id, NQ)
    z = zh * NZ + zl

    def plane_peer(dx, dq):
        return (lax.rem(x + dx, NX) * NZ + zl, zh * NQ + lax.rem(q + dq, NQ))

    def ring_peer(dz):
        far = lax.rem(z + dz, RING)
        return (x * NZ + lax.rem(far, NZ), lax.div(far, NZ) * NQ + q)

    def low_peer(dz):
        return (x * NZ + lax.rem(zl + dz, NZ), o_id)

    def send(src, dst, ssem, rsem, peer):
        pltpu.make_async_remote_copy(
            src_ref=src, dst_ref=dst, send_sem=ssem, recv_sem=rsem,
            device_id=peer, device_id_type=MESH,
        ).start()

    def finish(buf, ssem, rsem, peer):
        copy = pltpu.make_async_remote_copy(
            src_ref=buf, dst_ref=buf, send_sem=ssem, recv_sem=rsem,
            device_id=peer, device_id_type=MESH,
        )
        copy.wait_send()
        copy.wait_recv()

    load = pltpu.make_async_copy(pat_hbm, pat, in_sem)
    load.start()

    barrier = pltpu.get_barrier_semaphore()

    @pl.loop(1, PLANE)
    def _(j):
        pl.semaphore_signal(
            barrier, inc=1, device_id=plane_peer(lax.div(j, NQ), lax.rem(j, NQ)),
            device_id_type=MESH,
        )

    @pl.loop(1, RING)
    def _(j):
        pl.semaphore_signal(barrier, inc=1, device_id=ring_peer(j), device_id_type=MESH)

    row = lax.broadcasted_iota(jnp.int32, (8, 128), 0)
    lane = lax.broadcasted_iota(jnp.int32, (8, 128), 1)
    diag = jnp.where(lax.div(lane, DEG) == row, 1.0, 0.0).astype(F32)

    @pl.loop(0, ORD // 8)
    def _(g):
        cols = pl.ds(pl.multiple_of(g * 128, 128), 128)
        m = model_ref[:, cols]
        high = m.astype(BF16).astype(F32)
        low = m - high
        left = jnp.concatenate(
            [
                (high[:, None, :] * diag[None]).reshape(512, 128).astype(BF16),
                (low[:, None, :] * diag[None]).reshape(512, 128).astype(BF16),
            ],
            axis=1,
        )
        w = wig_ref[:, cols]
        out = lax.dot_general(
            left, jnp.concatenate([w, w], axis=1), (((1,), (1,)), ((), ())),
            preferred_element_type=F32,
        )
        cyc[:, pl.ds(pl.multiple_of(g * 8, 8), 8), :] = out.reshape(RADII, 8, OWN_R)

    def expand(j, total):
        c = cyc[pl.ds(j * 4, 4)].reshape(BLK, OWN_R)
        value = (BACKGROUND + apply_table(syn_ref, c)).astype(BF16)
        logs[pl.ds(pl.multiple_of(j * BLK, BLK), BLK), :] = value
        e = jnp.exp(value.astype(F32))
        return total + jnp.sum(e.reshape(BLK // 8, 8, OWN_R), axis=0)

    total = lax.fori_loop(0, NBLK, expand, jnp.zeros((8, OWN_R), F32))
    intensity = jnp.sum(total, axis=0, keepdims=True)

    load.wait()
    prod = dot(pat[...], logs[...])
    scaled = TEMPER * (prod - intensity)
    for t in range(PT):
        score[t] = scaled[t * 128:(t + 1) * 128, :].T
    peaks, masses = [], []
    for t in range(PT):
        s = score[t]
        m = jnp.max(s, axis=0, keepdims=True)
        peaks.append(m)
        masses.append(jnp.sum(jnp.exp(s - m), axis=0, keepdims=True))
    blank = jnp.zeros((8 - 2 * PT, 128), F32)
    stat[...] = jnp.concatenate(peaks + masses + [blank], axis=0)

    pl.semaphore_wait(barrier, PLANE - 1 + RING - 1)

    @pl.loop(1, NQ)
    def _(j):
        send(stat, b1.at[j - 1], b1_s, b1_r, plane_peer(0, j))

    low_half = lax.broadcasted_iota(jnp.int32, (OWN_R, 128), 1) < 64
    for t in range(NQ // 2):
        a = wig_ref[:, t * 128:(t + 1) * 128].astype(F32)
        b = wig_ref[:, 512 + t * 128:512 + (t + 1) * 128].astype(F32)
        wig_p[2 * t] = jnp.where(low_half, a, pltpu.roll(b, 64, 1)).astype(BF16)
        wig_p[2 * t + 1] = jnp.where(low_half, pltpu.roll(a, 64, 1), b).astype(BF16)

    finish(b1, b1_s, b1_r, plane_peer(0, 1))
    peak = stat[0:PT, :]
    for j in range(NQ - 1):
        peak = jnp.maximum(peak, b1[j, 0:PT, :])
    mass = stat[PT:2 * PT, :] * jnp.exp(stat[0:PT, :] - peak)
    for j in range(NQ - 1):
        mass = mass + b1[j, PT:2 * PT, :] * jnp.exp(b1[j, 0:PT, :] - peak)
    pair[...] = jnp.concatenate([peak, mass, blank], axis=0)
    send(pair, b2, b2_s, b2_r, ring_peer(NZ))

    @pl.loop(0, PIX // 128)
    def _(j):
        span = pl.ds(pl.multiple_of(j * 128, 128), 128)
        pat_t[span, :] = pat[:, span].T

    finish(b2, b2_s, b2_r, ring_peer(NZ))
    far_peak = b2[0:PT, :]
    top = jnp.maximum(peak, far_peak)
    mass = mass * jnp.exp(peak - top) + b2[PT:2 * PT, :] * jnp.exp(far_peak - top)
    part = jnp.zeros((8, OWN_R), F32)
    for t in range(PT):
        factor = mask_ref[:, t * 128:(t + 1) * 128].astype(F32) / mass[t:t + 1, :]
        w = (jnp.exp(score[t] - top[t:t + 1, :]) * factor).T.astype(BF16)
        wt[t * 128:(t + 1) * 128, :] = w
        part = part + jnp.sum(w.astype(F32).reshape(16, 8, OWN_R), axis=0)
    occ1[...] = jnp.sum(part, axis=0, keepdims=True)

    @pl.loop(1, NX)
    def _(j):
        send(occ1, c1.at[j - 1], c1_s, c1_r, plane_peer(j, 0))

    def compress(j, carry):
        rows = pl.ds(pl.multiple_of(j * BLK, BLK), BLK)
        ordt[rows, :] = apply_table(fwd_ref, dot(pat_t[rows, :], wt[...]))
        return carry

    lax.fori_loop(0, NBLK // 2, compress, 0)
    finish(c1, c1_s, c1_r, plane_peer(1, 0))
    occ = occ1[...]
    for j in range(NX - 1):
        occ = occ + c1[j]
    occ2[...] = occ

    @pl.loop(1, NZ)
    def _(j):
        send(occ2, c2.at[j - 1], c2_s, c2_r, low_peer(j))

    lax.fori_loop(NBLK // 2, NBLK, compress, 0)
    finish(c2, c2_s, c2_r, low_peer(1))
    for j in range(NZ - 1):
        occ = occ + c2[j]
    inv = (1.0 / math.sqrt(ORIENTS)) / (occ + 1.0)

    slot = lax.div(lax.broadcasted_iota(jnp.int32, (RADII, 128), 1), DEG)

    def project(i, carry):
        g = lax.rem(q + i, NQ)
        lefts = []
        for kk in range(8):
            k = (kk // 4) * (ORD // 2) + g * 4 + kk % 4
            o = ordt[pl.ds(k, RADII, stride=ORD), :] * inv
            high, low = split(o)
            lefts.append(jnp.concatenate([high, low], axis=1))
        w = wig_p[g]
        out = dot(jnp.concatenate(lefts, axis=0), jnp.concatenate([w, w], axis=0))
        acc = jnp.zeros((RADII, 128), F32)
        for kk in range(8):
            acc = jnp.where(slot == kk, out[kk * RADII:(kk + 1) * RADII, :], acc)
        harm[g] = acc.reshape(NX, 16, 128)

        for dx in range(NX):
            far = lax.rem(x + dx, NX)
            n = dx * NQ + i

            @pl.when(n > 0)
            def _():
                send(
                    harm.at[g, far], e1.at[jnp.maximum(n - 1, 0)], e1_s, e1_r,
                    plane_peer(dx, i),
                )
        return carry

    lax.fori_loop(0, NQ, project, 0)
    finish(e1, e1_s, e1_r, plane_peer(1, 0))
    tot = harm[q, x]
    for j in range(PLANE - 1):
        tot = tot + e1[j]
    zsum[...] = tot
    even = zsum[pl.ds(0, 8, stride=2), :]
    odd = zsum[pl.ds(1, 8, stride=2), :]
    first = lane < 64
    rows = jnp.concatenate(
        [
            jnp.where(first, even, pltpu.roll(odd, 64, 1)),
            jnp.where(first, pltpu.roll(even, 64, 1), odd),
        ],
        axis=0,
    )
    for j in range(RING):
        zsend[j] = rows[j:j + 1, :]

    @pl.loop(1, RING)
    def _(j):
        send(zsend.at[lax.rem(z + j, RING)], e2.at[j - 1], e2_s, e2_r, ring_peer(j))

    finish(e2, e2_s, e2_r, ring_peer(1))
    fin = zsend[z]
    for j in range(RING - 1):
        fin = fin + e2[j]
    out_ref[0:1, :] = fin[:, :64]
    out_ref[1:2, :] = fin[:, 64:]


def local(patterns, mask, model, wigner):
    table = order_table()
    syn = jnp.asarray(two_terms(table.T))
    fwd = jnp.asarray(two_terms(table * (2.0 / ANGLES)))
    vmem = pl.BlockSpec(memory_space=pltpu.VMEM)
    dma = pltpu.SemaphoreType.DMA
    out = pl.pallas_call(
        kernel,
        out_shape=jax.ShapeDtypeStruct((2, 64), F32),
        in_specs=[pl.BlockSpec(memory_space=pl.ANY)] + [vmem] * 5,
        out_specs=vmem,
        scratch_shapes=[
            pltpu.VMEM((OWN_P, PIX), BF16),
            pltpu.VMEM((PIX, OWN_P), BF16),
            pltpu.VMEM((RADII, ORD, OWN_R), F32),
            pltpu.VMEM((PIX, OWN_R), BF16),
            pltpu.VMEM((PT, OWN_R, 128), F32),
            pltpu.VMEM((NQ, OWN_R, 128), BF16),
            pltpu.VMEM((OWN_P, OWN_R), BF16),
            pltpu.VMEM((PIX, OWN_R), F32),
            pltpu.VMEM((8, 128), F32),
            pltpu.VMEM((NQ - 1, 8, 128), F32),
            pltpu.VMEM((8, 128), F32),
            pltpu.VMEM((8, 128), F32),
            pltpu.VMEM((1, 128), F32),
            pltpu.VMEM((NX - 1, 1, 128), F32),
            pltpu.VMEM((1, 128), F32),
            pltpu.VMEM((NZ - 1, 1, 128), F32),
            pltpu.VMEM((NQ, NX, 16, 128), F32),
            pltpu.VMEM((PLANE - 1, 16, 128), F32),
            pltpu.VMEM((16, 128), F32),
            pltpu.VMEM((RING, 1, 128), F32),
            pltpu.VMEM((RING - 1, 1, 128), F32),
        ]
        + [dma(())] * 13,
        compiler_params=pltpu.CompilerParams(collective_id=0, has_side_effects=True),
        name="recover",
    )(patterns, mask.reshape(1, OWN_P), model.T, wigner, syn, fwd)
    return out.T


def solution(mesh):
    return jax.shard_map(
        local,
        mesh=mesh,
        in_specs=(P("pat", None), P("pat"), P(), P("ori", None)),
        out_specs=P("ori", "pat"),
        check_vma=False,
    )
```

time: 433 us -> 56.3 us (0.13)
  blocking collectives: 249 us -> 0 us
  waiting for transfers between devices: 114 us -> 0 us
  Pallas kernels: 0 us -> 53.7 us
  starting transfers between devices: 35.3 us -> 0 us
  between operations: 13.5 us -> 0.01 us
  matrix products: 11.2 us -> 0 us
  local copies, waits for them, and re-layouts: 8.91 us -> 2.5 us
    psum x2 -> x0, blocking collectives: 181 us -> none  [the longest x1 109 us: local(): occupancy = lax.psum(jnp.sum(weights.astype(jnp.float32), axis=0), 'pat')]
    reduce_scatter x1 -> x0, waiting for transfers between devices: 101 us -> none  [local(): lax.psum_scatter(lax.dot_general(patterns, weights, contract_first, prefe...]
    pmax x1 -> x0, blocking collectives: 68.2 us -> none  [local(): row_peak = lax.pmax(local_peak, 'ori')]
    pallas_call x0 -> x1, Pallas kernels: none -> 53.7 us  [local(): pl.pallas_call(kernel, out_shape=jax.ShapeDtypeStruct((2, 64), F32), in_s...]
    all_to_all x2 -> x0, starting transfers between devices: 35.3 us -> none  [the longest x1 30.7 us: local(): lax.all_to_all(cycle_data, 'ori', split_axis=0, concat_axis=2, tiled=True)]
    all_to_all x2 -> x0, waiting for transfers between devices: 12.6 us -> none  [the longest x1 12.6 us: local(): lax.all_to_all(cycle_data, 'ori', split_axis=0, concat_axis=2, tiled=True)]
    dot_general x6 -> x0, matrix products: 11.2 us -> none  [the longest x1 3.65 us: local(): jnp.einsum('kbr,ka->bar', cycle_model, synthesis, precision=highest)]
    unnamed x9 -> x1, local copies, waits for them, and re-layouts: 5.6 us -> 1.22 us
  transfers between devices with their start and end apart: 3 -> 0, of which waited for: 2 -> 0; matrix products, arithmetic and copies ran while one was open for 1% -> 0% of each run, Pallas kernels for 0% -> 0%
where the time goes in v1:
time: 56.3 us; the launch traced here: 56.2 us
  Pallas kernels  53.7 us (95%)
  local copies, waits for them, and re-layouts  2.5 us (4%)
    pallas_call x1, Pallas kernels, local(): pl.pallas_call(kernel, out_shape=jax.ShapeDtypeStruct((2, 64), F32), in_s...  53.7 us
    reshape x1, local copies, waits for them, and re-layouts, local(): mask.reshape(1, OWN_P)  1.27 us
    unnamed x1, local copies, waits for them, and re-layouts  1.22 us

profile of v1, /device:TPU:1, one launch (start us, length us, event | category | flops | bytes accessed | tf_op | source)
XLA Modules:
  0.0 56.2 jit_solution(2476341464447315910)
XLA Ops:
  0.0 1.3 %reshape.3.mask_ref = s32[1,384]{1,0:T(1,128)} reshape(s32[384]{0:T(512)} %param.7) | data formatting | bytes 3072 | tf_op jit(solution)/shard_map/reshape | solution.py:334
  1.3 53.7 %recover.1 = f32[2,64]{1,0:T(2,128)} custom-call(bf16[384,4096]{1,0:T(8,128)(2,1)} %pat_hbm.1, s32[1,384]{1,0:T(1,128)} %reshape.3.mask_ref, f32[64,1024]{1,0:T(8,128)} %bitcast.2, bf16[128,1024]{1,0:T(8,128)(2,1)} %wig_ref.1, bf16[2,256,256]{2,1,0:T(8,128)(2,1)} %constant.4.clone.syn_ref, bf16[2,256,256]{2,1,0:T(8,128)(2,1)} %constant.5.clone.fwd_ref), custom_call_target="tpu_custom_call" | custom-call | tf_op jit(solution)/shard_map/recover/pallas_call | solution.py:303
  54.9 1.2 %copy.8 = f32[64,2]{0,1:T(2,128)} copy(f32[64,2]{0,1:T(2,128)} %bitcast.3) | data formatting | bytes 1024

commit v2 on v1

v2 whole, which is shorter than its diff:
```python
import math

import jax
import jax.numpy as jnp
import numpy as np
from jax import lax
from jax.experimental import pallas as pl
from jax.experimental.pallas import tpu as pltpu
from jax.sharding import PartitionSpec as P

RADII = 64
ANGLES = 64
DEG = 16
ORD = 64
PIX = 4096
HARM = 1024
PATTERNS = 12288
ORIENTS = 2048

TEMPER = 0.05
BACKGROUND = 0.1

NX, NZ = 4, 8
NH, NQ = 2, 8
PLANE = NX * NQ
RING = NH * NZ
OWN_P = PATTERNS // (NX * NZ)
OWN_R = ORIENTS // (NH * NQ)
PT = OWN_P // 128
BLK = 4 * ANGLES
NBLK = PIX // BLK

F32 = jnp.float32
BF16 = jnp.bfloat16
MESH = pl.DeviceIdType.MESH


def order_table():
    orders = np.arange(ORD)[:, None]
    angles = np.arange(ANGLES)[None, :]
    half = ANGLES // 2
    step = 2.0 * math.pi / ANGLES
    cos = np.cos(step * ((orders * angles) % ANGLES))
    sin = np.sin(step * (((orders - half) * angles) % ANGLES))
    return np.where(orders <= half, cos, sin).astype(np.float32)


def two_terms(full):
    high = full.astype(BF16)
    low = (full - high.astype(np.float32)).astype(BF16)
    return np.stack([high, low])


def tables():
    table = order_table()
    eye = np.eye(4, dtype=np.float32)
    syn = np.einsum("ka,bc->bakc", table, eye).reshape(BLK, BLK)
    fwd = np.einsum("ka,bc->kbca", table * np.float32(2.0 / ANGLES), eye)
    swap = fwd[np.arange(ORD) ^ 1]
    return (
        two_terms(syn),
        np.stack([two_terms(fwd.reshape(BLK, BLK)), two_terms(swap.reshape(BLK, BLK))]),
    )


def split(value):
    high = value.astype(BF16)
    low = (value - high.astype(F32)).astype(BF16)
    return high, low


def dot(a, b):
    return jnp.dot(a, b, preferred_element_type=F32)


def apply_table(table_ref, value):
    high, low = split(value)
    both = dot(table_ref[0], jnp.concatenate([high, low], axis=1))
    return both[:, :OWN_R] + both[:, OWN_R:] + dot(table_ref[1], high)


def far_first(n):
    return sorted(range(1, n), key=lambda j: -min(j, n - j))


def kernel(
    pat_hbm, mask_hbm, model_hbm, wig_hbm, syn_hbm, fwd_hbm, out_ref,
    pat, mask, model, wig, syn, fwd,
    pat_t, cyc, logs, score, wig_p, wt, ordt,
    stat, b1, pair, b2, occ1, c1, occ2, c2, harm, e1, zsum, zsend, e2,
    pat_sem, mask_sem, model_sem, wig_sem, syn_sem, fwd_sem,
    b1_s, b1_r, b2_s, b2_r, c1_s, c1_r, c2_s, c2_r, e1_s, e1_r, e2_s, e2_r,
):
    p_id = lax.axis_index("pat")
    o_id = lax.axis_index("ori")
    x, zl = lax.div(p_id, NZ), lax.rem(p_id, NZ)
    zh, q = lax.div(o_id, NQ), lax.rem(o_id, NQ)
    z = zh * NZ + zl

    def plane_peer(dx, dq):
        return (lax.rem(x + dx, NX) * NZ + zl, zh * NQ + lax.rem(q + dq, NQ))

    def ring_peer(dz):
        far = lax.rem(z + dz, RING)
        return (x * NZ + lax.rem(far, NZ), lax.div(far, NZ) * NQ + q)

    def low_peer(dz):
        return (x * NZ + lax.rem(zl + dz, NZ), o_id)

    def greet(peer):
        pl.semaphore_signal(barrier, inc=1, device_id=peer, device_id_type=MESH)

    def send(src, dst, ssem, rsem, peer):
        pltpu.make_async_remote_copy(
            src_ref=src, dst_ref=dst, send_sem=ssem, recv_sem=rsem,
            device_id=peer, device_id_type=MESH,
        ).start()

    def finish(buf, ssem, rsem, peer):
        copy = pltpu.make_async_remote_copy(
            src_ref=buf, dst_ref=buf, send_sem=ssem, recv_sem=rsem,
            device_id=peer, device_id_type=MESH,
        )
        copy.wait_send()
        copy.wait_recv()

    loads = [
        pltpu.make_async_copy(*refs)
        for refs in (
            (model_hbm, model, model_sem), (wig_hbm, wig, wig_sem), (syn_hbm, syn, syn_sem),
            (pat_hbm, pat, pat_sem), (fwd_hbm, fwd, fwd_sem), (mask_hbm, mask, mask_sem),
        )
    ]
    model_in, wig_in, syn_in, pat_in, fwd_in, mask_in = loads
    for load in loads:
        load.start()

    barrier = pltpu.get_barrier_semaphore()
    greet(ring_peer(NZ))
    for j in far_first(NZ):
        greet(low_peer(j))
    for j in far_first(NX):
        greet(plane_peer(j, 0))
    for j in far_first(NQ):
        greet(plane_peer(0, j))

    row = lax.broadcasted_iota(jnp.int32, (16, 128), 0)
    lane = lax.broadcasted_iota(jnp.int32, (16, 128), 1)
    own = [
        jnp.where(lax.div(lane, DEG) == lax.div(row, 4) + n, 1.0, 0.0).astype(BF16)
        for n in (0, 4)
    ]
    upper = lax.broadcasted_iota(jnp.int32, (1, 8, 128), 1) < 4
    model_in.wait()
    wig_in.wait()

    def spread(value):
        tile = value.reshape(RADII // 8, 8, 128)
        other = pltpu.roll(tile, 4, 1)
        one = jnp.where(upper, tile, other)
        two = jnp.where(upper, other, tile)
        rows = []
        for i in range(RADII // 8):
            for half in (one[i], two[i]):
                packed = jnp.concatenate([half, half], axis=0).astype(BF16)
                rows += [packed * own[0], packed * own[1]]
        return jnp.concatenate(rows, axis=0)

    def gather_cycles(g):
        cols = pl.ds(pl.multiple_of(g * 128, 128), 128)
        m = model[:, cols]
        high = m.astype(BF16).astype(F32)
        left = jnp.concatenate([spread(high), spread(m - high)], axis=1)
        w = wig[:, cols]
        out = lax.dot_general(
            left, jnp.concatenate([w, w], axis=1), (((1,), (1,)), ((), ())),
            preferred_element_type=F32,
        )
        cyc[:, pl.ds(pl.multiple_of(g * 32, 32), 32), :] = out.reshape(NBLK, 32, OWN_R)

    @pl.loop(0, ORD // 16)
    def _(g):
        gather_cycles(2 * g)
        gather_cycles(2 * g + 1)

    syn_in.wait()

    def expand(j, total):
        value = (BACKGROUND + apply_table(syn, cyc[j])).astype(BF16)
        logs[pl.ds(pl.multiple_of(j * BLK, BLK), BLK), :] = value
        e = jnp.exp(value.astype(F32))
        return total + jnp.sum(e.reshape(BLK // 8, 8, OWN_R), axis=0)

    def expand_four(j, total):
        for n in range(4):
            total = expand(4 * j + n, total)
        return total

    total = lax.fori_loop(0, NBLK // 4, expand_four, jnp.zeros((8, OWN_R), F32))
    intensity = jnp.sum(total, axis=0, keepdims=True)

    pat_in.wait()
    scaled = TEMPER * (dot(pat[...], logs[...]) - intensity)
    for t in range(PT):
        score[t] = scaled[t * 128:(t + 1) * 128, :].T
    peaks, masses = [], []
    for t in range(PT):
        s = score[t]
        m = jnp.max(s, axis=0, keepdims=True)
        peaks.append(m)
        masses.append(jnp.sum(jnp.exp(s - m), axis=0, keepdims=True))
    blank = jnp.zeros((8 - 2 * PT, 128), F32)
    stat[...] = jnp.concatenate(peaks + masses + [blank], axis=0)

    pl.semaphore_wait(barrier, 1 + NZ - 1 + NX - 1 + NQ - 1)

    for j in far_first(NQ):
        send(stat, b1.at[j - 1], b1_s, b1_r, plane_peer(0, j))

    fwd_in.wait()
    mask_in.wait()
    low_half = lax.broadcasted_iota(jnp.int32, (OWN_R, 128), 1) < 64
    for t in range(NQ // 2):
        a = wig[:, t * 128:(t + 1) * 128].astype(F32)
        b = wig[:, 512 + t * 128:512 + (t + 1) * 128].astype(F32)
        wig_p[2 * t] = jnp.where(low_half, a, pltpu.roll(b, 64, 1)).astype(BF16)
        wig_p[2 * t + 1] = jnp.where(low_half, pltpu.roll(a, 64, 1), b).astype(BF16)

    finish(b1, b1_s, b1_r, plane_peer(0, 1))
    peak = stat[0:PT, :]
    for j in range(NQ - 1):
        peak = jnp.maximum(peak, b1[j, 0:PT, :])
    mass = stat[PT:2 * PT, :] * jnp.exp(stat[0:PT, :] - peak)
    for j in range(NQ - 1):
        mass = mass + b1[j, PT:2 * PT, :] * jnp.exp(b1[j, 0:PT, :] - peak)
    pair[...] = jnp.concatenate([peak, mass, blank], axis=0)
    send(pair, b2, b2_s, b2_r, ring_peer(NZ))

    @pl.loop(0, PIX // 128)
    def _(j):
        span = pl.ds(pl.multiple_of(j * 128, 128), 128)
        pat_t[span, :] = pat[:, span].T

    finish(b2, b2_s, b2_r, ring_peer(NZ))
    far_peak = b2[0:PT, :]
    top = jnp.maximum(peak, far_peak)
    mass = mass * jnp.exp(peak - top) + b2[PT:2 * PT, :] * jnp.exp(far_peak - top)
    part = jnp.zeros((8, OWN_R), F32)
    for t in range(PT):
        counts = mask[t * 128:(t + 1) * 128].astype(F32).reshape(1, 128)
        factor = counts / mass[t:t + 1, :]
        w = (jnp.exp(score[t] - top[t:t + 1, :]) * factor).T.astype(BF16)
        wt[t * 128:(t + 1) * 128, :] = w
        part = part + jnp.sum(w.astype(F32).reshape(16, 8, OWN_R), axis=0)
    occ1[...] = jnp.sum(part, axis=0, keepdims=True)

    for j in far_first(NX):
        send(occ1, c1.at[j - 1], c1_s, c1_r, plane_peer(j, 0))

    def compress(i, carry):
        parts = []
        for n in range(2):
            rows = pl.ds(pl.multiple_of((2 * i + n) * BLK, BLK), BLK)
            parts.append(
                apply_table(fwd.at[n], dot(pat_t[rows, :], wt[...])).reshape(ORD // 2, 8, OWN_R)
            )
        cols = pl.ds(pl.multiple_of(i * 8, 8), 8)
        ordt[:, 0, cols, :] = jnp.where(upper, parts[0], parts[1])
        ordt[:, 1, cols, :] = jnp.where(upper, parts[1], parts[0])
        return carry

    lax.fori_loop(0, 2, compress, 0)
    finish(c1, c1_s, c1_r, plane_peer(1, 0))
    occ = occ1[...]
    for j in range(NX - 1):
        occ = occ + c1[j]
    occ2[...] = occ

    for j in far_first(NZ):
        send(occ2, c2.at[j - 1], c2_s, c2_r, low_peer(j))

    lax.fori_loop(2, NBLK // 2, compress, 0)
    finish(c2, c2_s, c2_r, low_peer(1))
    for j in range(NZ - 1):
        occ = occ + c2[j]
    inv = (1.0 / math.sqrt(ORIENTS)) / (occ + 1.0)

    slot = lax.div(lax.broadcasted_iota(jnp.int32, (RADII, 128), 1), DEG)

    def project(i):
        g = lax.rem(q + i, NQ)
        lefts = []
        for kk in range(8):
            o = ordt[(kk // 4) * (ORD // 4) + g * 2 + (kk % 4) // 2, kk % 2] * inv
            high, low = split(o)
            lefts.append(jnp.concatenate([high, low], axis=1))
        w = wig_p[g]
        out = dot(jnp.concatenate(lefts, axis=0), jnp.concatenate([w, w], axis=0))
        acc = [jnp.zeros((RADII, 128), F32)] * 2
        for kk in range(8):
            acc[kk % 2] = jnp.where(slot == kk, out[kk * RADII:(kk + 1) * RADII, :], acc[kk % 2])
        odd = pltpu.roll(acc[1].reshape(RADII // 8, 8, 128), 4, 1).reshape(RADII, 128)
        harm[g] = (acc[0] + odd).astype(BF16).reshape(NX, 16, 128)
        for dx in (2, 1, 3, 0):
            if dx or i:
                send(
                    harm.at[g, lax.rem(x + dx, NX)], e1.at[dx * NQ + i - 1], e1_s, e1_r,
                    plane_peer(dx, i),
                )

    for i in far_first(NQ) + [0]:
        project(i)
    finish(e1, e1_s, e1_r, plane_peer(1, 0))
    tot = harm[q, x].astype(F32)
    for j in range(PLANE - 1):
        tot = tot + e1[j].astype(F32)
    zsum[...] = tot
    even = zsum[pl.ds(0, 8, stride=2), :]
    odd = zsum[pl.ds(1, 8, stride=2), :]
    first = lane[:8] < 64
    rows = jnp.concatenate(
        [
            jnp.where(first, even, pltpu.roll(odd, 64, 1)),
            jnp.where(first, pltpu.roll(even, 64, 1), odd),
        ],
        axis=0,
    )
    for j in range(RING):
        zsend[j] = rows[j:j + 1, :]
    for j in far_first(RING):
        send(zsend.at[lax.rem(z + j, RING)], e2.at[j - 1], e2_s, e2_r, ring_peer(j))
    finish(e2, e2_s, e2_r, ring_peer(1))
    fin = zsend[z]
    for j in range(RING - 1):
        fin = fin + e2[j]
    out_ref[0:1, :] = fin[:, :64]
    out_ref[1:2, :] = fin[:, 64:]


def local(patterns, mask, model, wigner):
    syn, fwd = tables()
    hbm = pl.BlockSpec(memory_space=pl.ANY)
    dma = pltpu.SemaphoreType.DMA
    out = pl.pallas_call(
        kernel,
        out_shape=jax.ShapeDtypeStruct((2, 64), F32),
        in_specs=[hbm] * 6,
        out_specs=pl.BlockSpec(memory_space=pltpu.VMEM),
        scratch_shapes=[
            pltpu.VMEM((OWN_P, PIX), BF16),
            pltpu.VMEM((OWN_P,), jnp.int32),
            pltpu.VMEM((RADII, HARM), F32),
            pltpu.VMEM((OWN_R, HARM), BF16),
            pltpu.VMEM(syn.shape, BF16),
            pltpu.VMEM(fwd.shape, BF16),
            pltpu.VMEM((PIX, OWN_P), BF16),
            pltpu.VMEM((NBLK, BLK, OWN_R), F32),
            pltpu.VMEM((PIX, OWN_R), BF16),
            pltpu.VMEM((PT, OWN_R, 128), F32),
            pltpu.VMEM((NQ, OWN_R, 128), BF16),
            pltpu.VMEM((OWN_P, OWN_R), BF16),
            pltpu.VMEM((ORD // 2, 2, RADII, OWN_R), F32),
            pltpu.VMEM((8, 128), F32),
            pltpu.VMEM((NQ - 1, 8, 128), F32),
            pltpu.VMEM((8, 128), F32),
            pltpu.VMEM((8, 128), F32),
            pltpu.VMEM((1, 128), F32),
            pltpu.VMEM((NX - 1, 1, 128), F32),
            pltpu.VMEM((1, 128), F32),
            pltpu.VMEM((NZ - 1, 1, 128), F32),
            pltpu.VMEM((NQ, NX, 16, 128), BF16),
            pltpu.VMEM((PLANE - 1, 16, 128), BF16),
            pltpu.VMEM((16, 128), F32),
            pltpu.VMEM((RING, 1, 128), F32),
            pltpu.VMEM((RING - 1, 1, 128), F32),
        ]
        + [dma(())] * 18,
        compiler_params=pltpu.CompilerParams(collective_id=0, has_side_effects=True),
        name="recover",
    )(patterns, mask, model.T, wigner, jnp.asarray(syn), jnp.asarray(fwd))
    return out.T


def solution(mesh):
    return jax.shard_map(
        local,
        mesh=mesh,
        in_specs=(P("pat", None), P("pat"), P(), P("ori", None)),
        out_specs=P("ori", "pat"),
        check_vma=False,
    )
```

time: 56.3 us -> 50.5 us (0.90)
  Pallas kernels: 53.7 us -> 49.1 us
  local copies, waits for them, and re-layouts: 2.5 us -> 1.24 us
    pallas_call x1, Pallas kernels: 53.7 us -> 49.1 us  [local(): pl.pallas_call(kernel, out_shape=jax.ShapeDtypeStruct((2, 64), F32), in_s...]
    reshape x1 -> x0, local copies, waits for them, and re-layouts: 1.27 us -> none  [local(): mask.reshape(1, OWN_P)]
where the time goes in v2:
time: 50.5 us; the launch traced here: 50.3 us
  Pallas kernels  49.1 us (97%)
  local copies, waits for them, and re-layouts  1.24 us (2%)
    pallas_call x1, Pallas kernels, local(): pl.pallas_call(kernel, out_shape=jax.ShapeDtypeStruct((2, 64), F32), in_s...  49.1 us
    unnamed x1, local copies, waits for them, and re-layouts  1.24 us

profile of v2, /device:TPU:1, one launch (start us, length us, event | category | flops | bytes accessed | tf_op | source)
XLA Modules:
  0.0 50.3 jit_solution(17931844764064540941)
XLA Ops:
  0.0 49.1 %recover.1 = f32[2,64]{1,0:T(2,128)} custom-call(bf16[384,4096]{1,0:T(8,128)(2,1)} %pat_hbm.1, s32[384]{0:T(512)} %mask_hbm.1, f32[64,1024]{1,0:T(8,128)} %bitcast.2, bf16[128,1024]{1,0:T(8,128)(2,1)} %wig_hbm.1, bf16[2,256,256]{2,1,0:T(8,128)(2,1)} %constant.4.clone.syn_hbm, bf16[2,2,256,256]{3,2,1,0:T(8,128)(2,1)} %constant.5.clone.fwd_hbm), custom_call_target="tpu_custom_call" | custom-call | tf_op jit(solution)/shard_map/recover/pallas_call | solution.py:344
  49.1 1.2 %copy.8 = f32[64,2]{0,1:T(2,128)} copy(f32[64,2]{0,1:T(2,128)} %bitcast.3) | data formatting | bytes 1024

commit v3 on v2

--- a/solution.py
+++ b/solution.py
@@ -45,10 +45,10 @@
     return np.where(orders <= half, cos, sin).astype(np.float32)
 
 
-def two_terms(full):
+def terms(full):
     high = full.astype(BF16)
     low = (full - high.astype(np.float32)).astype(BF16)
-    return np.stack([high, low])
+    return np.concatenate([high, high, low], axis=1)
 
 
 def tables():
@@ -58,8 +58,8 @@
     fwd = np.einsum("ka,bc->kbca", table * np.float32(2.0 / ANGLES), eye)
     swap = fwd[np.arange(ORD) ^ 1]
     return (
-        two_terms(syn),
-        np.stack([two_terms(fwd.reshape(BLK, BLK)), two_terms(swap.reshape(BLK, BLK))]),
+        terms(syn),
+        np.stack([terms(fwd.reshape(BLK, BLK)), terms(swap.reshape(BLK, BLK))]),
     )
 
 
@@ -73,10 +73,10 @@
     return jnp.dot(a, b, preferred_element_type=F32)
 
 
-def apply_table(table_ref, value):
-    high, low = split(value)
-    both = dot(table_ref[0], jnp.concatenate([high, low], axis=1))
-    return both[:, :OWN_R] + both[:, OWN_R:] + dot(table_ref[1], high)
+def apply_table(table, one, two):
+    high, low = split(jnp.concatenate([one, two], axis=1))
+    out = dot(table, jnp.concatenate([high, low, high], axis=0))
+    return out[:, :OWN_R], out[:, OWN_R:]
 
 
 def far_first(n):
@@ -87,9 +87,9 @@
     pat_hbm, mask_hbm, model_hbm, wig_hbm, syn_hbm, fwd_hbm, out_ref,
     pat, mask, model, wig, syn, fwd,
     pat_t, cyc, logs, score, wig_p, wt, ordt,
-    stat, b1, pair, b2, occ1, c1, occ2, c2, harm, e1, zsum, zsend, e2,
+    stat, b1, pair, b2, occ1, c1, harm, e1, zsum, zsend, e2,
     pat_sem, mask_sem, model_sem, wig_sem, syn_sem, fwd_sem,
-    b1_s, b1_r, b2_s, b2_r, c1_s, c1_r, c2_s, c2_r, e1_s, e1_r, e2_s, e2_r,
+    b1_s, b1_r, b2_s, b2_r, c1_s, c1_r, e1_s, e1_r, e2_s, e2_r,
 ):
     p_id = lax.axis_index("pat")
     o_id = lax.axis_index("ori")
@@ -104,8 +104,10 @@
         far = lax.rem(z + dz, RING)
         return (x * NZ + lax.rem(far, NZ), lax.div(far, NZ) * NQ + q)
 
-    def low_peer(dz):
-        return (x * NZ + lax.rem(zl + dz, NZ), o_id)
+    def pat_peer(dx, dz):
+        return (lax.rem(x + dx, NX) * NZ + lax.rem(zl + dz, NZ), o_id)
+
+    pat_peers = [(dx, dz) for dz in far_first(NZ) + [0] for dx in (2, 1, 3, 0) if dx or dz]
 
     def greet(peer):
         pl.semaphore_signal(barrier, inc=1, device_id=peer, device_id_type=MESH)
@@ -116,13 +118,11 @@
             device_id=peer, device_id_type=MESH,
         ).start()
 
-    def finish(buf, ssem, rsem, peer):
-        copy = pltpu.make_async_remote_copy(
+    def whole(buf, ssem, rsem, peer):
+        return pltpu.make_async_remote_copy(
             src_ref=buf, dst_ref=buf, send_sem=ssem, recv_sem=rsem,
             device_id=peer, device_id_type=MESH,
         )
-        copy.wait_send()
-        copy.wait_recv()
 
     loads = [
         pltpu.make_async_copy(*refs)
@@ -137,10 +137,8 @@
 
     barrier = pltpu.get_barrier_semaphore()
     greet(ring_peer(NZ))
-    for j in far_first(NZ):
-        greet(low_peer(j))
-    for j in far_first(NX):
-        greet(plane_peer(j, 0))
+    for dx, dz in pat_peers:
+        greet(pat_peer(dx, dz))
     for j in far_first(NQ):
         greet(plane_peer(0, j))
 
@@ -178,25 +176,24 @@
         )
         cyc[:, pl.ds(pl.multiple_of(g * 32, 32), 32), :] = out.reshape(NBLK, 32, OWN_R)
 
-    @pl.loop(0, ORD // 16)
-    def _(g):
-        gather_cycles(2 * g)
-        gather_cycles(2 * g + 1)
+    @pl.loop(0, 2)
+    def _(h):
+        for n in range(ORD // 16):
+            gather_cycles(h * (ORD // 16) + n)
 
     syn_in.wait()
 
-    def expand(j, total):
-        value = (BACKGROUND + apply_table(syn, cyc[j])).astype(BF16)
-        logs[pl.ds(pl.multiple_of(j * BLK, BLK), BLK), :] = value
-        e = jnp.exp(value.astype(F32))
-        return total + jnp.sum(e.reshape(BLK // 8, 8, OWN_R), axis=0)
-
-    def expand_four(j, total):
-        for n in range(4):
-            total = expand(4 * j + n, total)
+    def expand(h, total):
+        for m in range(0, NBLK // 2, 2):
+            j = h * (NBLK // 2) + m
+            for n, part in enumerate(apply_table(syn[...], cyc[j], cyc[j + 1])):
+                value = (BACKGROUND + part).astype(BF16)
+                logs[pl.ds(pl.multiple_of((j + n) * BLK, BLK), BLK), :] = value
+                e = jnp.exp(value.astype(F32))
+                total = total + jnp.sum(e.reshape(BLK // 8, 8, OWN_R), axis=0)
         return total
 
-    total = lax.fori_loop(0, NBLK // 4, expand_four, jnp.zeros((8, OWN_R), F32))
+    total = lax.fori_loop(0, 2, expand, jnp.zeros((8, OWN_R), F32))
     intensity = jnp.sum(total, axis=0, keepdims=True)
 
     pat_in.wait()
@@ -212,7 +209,7 @@
     blank = jnp.zeros((8 - 2 * PT, 128), F32)
     stat[...] = jnp.concatenate(peaks + masses + [blank], axis=0)
 
-    pl.semaphore_wait(barrier, 1 + NZ - 1 + NX - 1 + NQ - 1)
+    pl.semaphore_wait(barrier, 1 + NX * NZ - 1 + NQ - 1)
 
     for j in far_first(NQ):
         send(stat, b1.at[j - 1], b1_s, b1_r, plane_peer(0, j))
@@ -226,7 +223,8 @@
         wig_p[2 * t] = jnp.where(low_half, a, pltpu.roll(b, 64, 1)).astype(BF16)
         wig_p[2 * t + 1] = jnp.where(low_half, pltpu.roll(a, 64, 1), b).astype(BF16)
 
-    finish(b1, b1_s, b1_r, plane_peer(0, 1))
+    b1_all = whole(b1, b1_s, b1_r, plane_peer(0, 1))
+    b1_all.wait_recv()
     peak = stat[0:PT, :]
     for j in range(NQ - 1):
         peak = jnp.maximum(peak, b1[j, 0:PT, :])
@@ -241,7 +239,8 @@
         span = pl.ds(pl.multiple_of(j * 128, 128), 128)
         pat_t[span, :] = pat[:, span].T
 
-    finish(b2, b2_s, b2_r, ring_peer(NZ))
+    b2_all = whole(b2, b2_s, b2_r, ring_peer(NZ))
+    b2_all.wait_recv()
     far_peak = b2[0:PT, :]
     top = jnp.maximum(peak, far_peak)
     mass = mass * jnp.exp(peak - top) + b2[PT:2 * PT, :] * jnp.exp(far_peak - top)
@@ -254,48 +253,51 @@
         part = part + jnp.sum(w.astype(F32).reshape(16, 8, OWN_R), axis=0)
     occ1[...] = jnp.sum(part, axis=0, keepdims=True)
 
-    for j in far_first(NX):
-        send(occ1, c1.at[j - 1], c1_s, c1_r, plane_peer(j, 0))
+    for dx, dz in pat_peers:
+        send(occ1, c1.at[dx * NZ + dz - 1], c1_s, c1_r, pat_peer(dx, dz))
 
     def compress(i, carry):
-        parts = []
-        for n in range(2):
-            rows = pl.ds(pl.multiple_of((2 * i + n) * BLK, BLK), BLK)
-            parts.append(
-                apply_table(fwd.at[n], dot(pat_t[rows, :], wt[...])).reshape(ORD // 2, 8, OWN_R)
+        rows = [pl.ds(pl.multiple_of((4 * i + n) * BLK, BLK), BLK) for n in range(4)]
+        sums = [dot(pat_t[r, :], wt[...]) for r in rows]
+        evens = apply_table(fwd[0], sums[0], sums[2])
+        odds = apply_table(fwd[1], sums[1], sums[3])
+        one, two = (
+            [v.reshape(ORD // 2, 8, OWN_R) for v in side] for side in (evens, odds)
+        )
+        cols = pl.ds(pl.multiple_of(i * 16, 16), 16)
+        for par in range(2):
+            whole_tile = jnp.concatenate(
+                [jnp.where(upper, *((a, b) if par == 0 else (b, a))) for a, b in zip(one, two)],
+                axis=1,
             )
-        cols = pl.ds(pl.multiple_of(i * 8, 8), 8)
-        ordt[:, 0, cols, :] = jnp.where(upper, parts[0], parts[1])
-        ordt[:, 1, cols, :] = jnp.where(upper, parts[1], parts[0])
+            high, low = split(whole_tile)
+            ordt[:, par, cols, 0:128] = high
+            ordt[:, par, cols, 128:256] = low
         return carry
 
-    lax.fori_loop(0, 2, compress, 0)
-    finish(c1, c1_s, c1_r, plane_peer(1, 0))
-    occ = occ1[...]
-    for j in range(NX - 1):
-        occ = occ + c1[j]
-    occ2[...] = occ
-
-    for j in far_first(NZ):
-        send(occ2, c2.at[j - 1], c2_s, c2_r, low_peer(j))
-
-    lax.fori_loop(2, NBLK // 2, compress, 0)
-    finish(c2, c2_s, c2_r, low_peer(1))
-    for j in range(NZ - 1):
-        occ = occ + c2[j]
+    lax.fori_loop(0, NBLK // 4, compress, 0)
+    c1_all = whole(c1, c1_s, c1_r, pat_peer(1, 0))
+    c1_all.wait_recv()
+    occ = occ1[...] + jnp.sum(c1[...], axis=0)
     inv = (1.0 / math.sqrt(ORIENTS)) / (occ + 1.0)
 
     slot = lax.div(lax.broadcasted_iota(jnp.int32, (RADII, 128), 1), DEG)
+
+    inv_rows = jnp.broadcast_to(inv, (OWN_R, OWN_R)).T
+    for n in range(NQ):
+        wig_p[n] = (wig_p[n].astype(F32) * inv_rows).astype(BF16)
 
     def project(i):
         g = lax.rem(q + i, NQ)
-        lefts = []
-        for kk in range(8):
-            o = ordt[(kk // 4) * (ORD // 4) + g * 2 + (kk % 4) // 2, kk % 2] * inv
-            high, low = split(o)
-            lefts.append(jnp.concatenate([high, low], axis=1))
         w = wig_p[g]
-        out = dot(jnp.concatenate(lefts, axis=0), jnp.concatenate([w, w], axis=0))
+        both = jnp.concatenate([w, w], axis=0)
+        left = [
+            ordt[pl.ds(h * (ORD // 4) + g * 2, 2)].reshape(BLK, 2 * OWN_R) for h in range(2)
+        ]
+        return dot(jnp.concatenate(left, axis=0), both)
+
+    def share(i, out):
+        g = lax.rem(q + i, NQ)
         acc = [jnp.zeros((RADII, 128), F32)] * 2
         for kk in range(8):
             acc[kk % 2] = jnp.where(slot == kk, out[kk * RADII:(kk + 1) * RADII, :], acc[kk % 2])
@@ -308,9 +310,14 @@
                     plane_peer(dx, i),
                 )
 
-    for i in far_first(NQ) + [0]:
-        project(i)
-    finish(e1, e1_s, e1_r, plane_peer(1, 0))
+    order = far_first(NQ) + [0]
+    out = project(order[0])
+    for i, later in zip(order, order[1:] + [None]):
+        coming = None if later is None else project(later)
+        share(i, out)
+        out = coming
+    e1_all = whole(e1, e1_s, e1_r, plane_peer(1, 0))
+    e1_all.wait_recv()
     tot = harm[q, x].astype(F32)
     for j in range(PLANE - 1):
         tot = tot + e1[j].astype(F32)
@@ -329,12 +336,19 @@
         zsend[j] = rows[j:j + 1, :]
     for j in far_first(RING):
         send(zsend.at[lax.rem(z + j, RING)], e2.at[j - 1], e2_s, e2_r, ring_peer(j))
-    finish(e2, e2_s, e2_r, ring_peer(1))
+    e2_all = whole(e2, e2_s, e2_r, ring_peer(1))
+    e2_all.wait_recv()
     fin = zsend[z]
     for j in range(RING - 1):
         fin = fin + e2[j]
     out_ref[0:1, :] = fin[:, :64]
     out_ref[1:2, :] = fin[:, 64:]
+    for copies in (b1_all, c1_all, e1_all, e2_all):
+        copies.wait_send()
+    pltpu.make_async_remote_copy(
+        src_ref=pair, dst_ref=b2, send_sem=b2_s, recv_sem=b2_r,
+        device_id=ring_peer(NZ), device_id_type=MESH,
+    ).wait_send()
 
 
 def local(patterns, mask, model, wigner):
@@ -359,22 +373,20 @@
             pltpu.VMEM((PT, OWN_R, 128), F32),
             pltpu.VMEM((NQ, OWN_R, 128), BF16),
             pltpu.VMEM((OWN_P, OWN_R), BF16),
-            pltpu.VMEM((ORD // 2, 2, RADII, OWN_R), F32),
+            pltpu.VMEM((ORD // 2, 2, RADII, 2 * OWN_R), BF16),
             pltpu.VMEM((8, 128), F32),
             pltpu.VMEM((NQ - 1, 8, 128), F32),
             pltpu.VMEM((8, 128), F32),
             pltpu.VMEM((8, 128), F32),
             pltpu.VMEM((1, 128), F32),
-            pltpu.VMEM((NX - 1, 1, 128), F32),
-            pltpu.VMEM((1, 128), F32),
-            pltpu.VMEM((NZ - 1, 1, 128), F32),
+            pltpu.VMEM((NX * NZ - 1, 1, 128), F32),
             pltpu.VMEM((NQ, NX, 16, 128), BF16),
             pltpu.VMEM((PLANE - 1, 16, 128), BF16),
             pltpu.VMEM((16, 128), F32),
             pltpu.VMEM((RING, 1, 128), F32),
             pltpu.VMEM((RING - 1, 1, 128), F32),
         ]
-        + [dma(())] * 18,
+        + [dma(())] * 16,
         compiler_params=pltpu.CompilerParams(collective_id=0, has_side_effects=True),
         name="recover",
     )(patterns, mask, model.T, wigner, jnp.asarray(syn), jnp.asarray(fwd))

time: 50.5 us -> 48 us (0.950)
  Pallas kernels: 49.1 us -> 46.6 us
    pallas_call x1, Pallas kernels: 49.1 us -> 46.6 us  [local(): pl.pallas_call(kernel, out_shape=jax.ShapeDtypeStruct((2, 64), F32), in_s...]
where the time goes in v3:
time: 48 us; the launch traced here: 47.9 us
  Pallas kernels  46.6 us (97%)
  local copies, waits for them, and re-layouts  1.24 us (3%)
    pallas_call x1, Pallas kernels, local(): pl.pallas_call(kernel, out_shape=jax.ShapeDtypeStruct((2, 64), F32), in_s...  46.6 us
    unnamed x1, local copies, waits for them, and re-layouts  1.24 us

profile of v3, /device:TPU:1, one launch (start us, length us, event | category | flops | bytes accessed | tf_op | source)
XLA Modules:
  0.0 47.9 jit_solution(14085438128735588818)
XLA Ops:
  0.0 46.6 %recover.1 = f32[2,64]{1,0:T(2,128)} custom-call(bf16[384,4096]{1,0:T(8,128)(2,1)} %pat_hbm.1, s32[384]{0:T(512)} %mask_hbm.1, f32[64,1024]{1,0:T(8,128)} %bitcast.2, bf16[128,1024]{1,0:T(8,128)(2,1)} %wig_hbm.1, bf16[256,768]{1,0:T(8,128)(2,1)} %constant.4.clone.syn_hbm, bf16[2,256,768]{2,1,0:T(8,128)(2,1)} %constant.5.clone.fwd_hbm), custom_call_target="tpu_custom_call" | custom-call | tf_op jit(solution)/shard_map/recover/pallas_call | solution.py:358
  46.6 1.2 %copy.8 = f32[64,2]{0,1:T(2,128)} copy(f32[64,2]{0,1:T(2,128)} %bitcast.3) | data formatting | bytes 1024

commit v4 on v3

--- a/solution.py
+++ b/solution.py
@@ -89,7 +89,7 @@
     pat_t, cyc, logs, score, wig_p, wt, ordt,
     stat, b1, pair, b2, occ1, c1, harm, e1, zsum, zsend, e2,
     pat_sem, mask_sem, model_sem, wig_sem, syn_sem, fwd_sem,
-    b1_s, b1_r, b2_s, b2_r, c1_s, c1_r, e1_s, e1_r, e2_s, e2_r,
+    b1_s, b1_r, b2_s, b2_r, c1_s, c1_r, e1_s, e1_r, e2_s, e2_r, known,
 ):
     p_id = lax.axis_index("pat")
     o_id = lax.axis_index("ori")
@@ -138,7 +138,8 @@
     barrier = pltpu.get_barrier_semaphore()
     greet(ring_peer(NZ))
     for dx, dz in pat_peers:
-        greet(pat_peer(dx, dz))
+        if dx == 0 or dz == 0:
+            greet(pat_peer(dx, dz))
     for j in far_first(NQ):
         greet(plane_peer(0, j))
 
@@ -209,10 +210,13 @@
     blank = jnp.zeros((8 - 2 * PT, 128), F32)
     stat[...] = jnp.concatenate(peaks + masses + [blank], axis=0)
 
-    pl.semaphore_wait(barrier, 1 + NX * NZ - 1 + NQ - 1)
+    pl.semaphore_wait(barrier, 1 + NX - 1 + NZ - 1 + NQ - 1)
 
     for j in far_first(NQ):
         send(stat, b1.at[j - 1], b1_s, b1_r, plane_peer(0, j))
+
+    for dx in far_first(NX):
+        pl.semaphore_signal(known, inc=1, device_id=pat_peer(dx, 0), device_id_type=MESH)
 
     fwd_in.wait()
     mask_in.wait()
@@ -253,6 +257,7 @@
         part = part + jnp.sum(w.astype(F32).reshape(16, 8, OWN_R), axis=0)
     occ1[...] = jnp.sum(part, axis=0, keepdims=True)
 
+    pl.semaphore_wait(known, NX - 1)
     for dx, dz in pat_peers:
         send(occ1, c1.at[dx * NZ + dz - 1], c1_s, c1_r, pat_peer(dx, dz))
 
@@ -270,9 +275,9 @@
                 [jnp.where(upper, *((a, b) if par == 0 else (b, a))) for a, b in zip(one, two)],
                 axis=1,
             )
-            high, low = split(whole_tile)
-            ordt[:, par, cols, 0:128] = high
-            ordt[:, par, cols, 128:256] = low
+            for h in range(NH):
+                half = whole_tile[h * (ORD // 4):(h + 1) * (ORD // 4)]
+                ordt[:, par, cols, h * OWN_R:(h + 1) * OWN_R] = half.astype(BF16)
         return carry
 
     lax.fori_loop(0, NBLK // 4, compress, 0)
@@ -281,25 +286,20 @@
     occ = occ1[...] + jnp.sum(c1[...], axis=0)
     inv = (1.0 / math.sqrt(ORIENTS)) / (occ + 1.0)
 
-    slot = lax.div(lax.broadcasted_iota(jnp.int32, (RADII, 128), 1), DEG)
+    slot = lax.rem(lax.div(lax.broadcasted_iota(jnp.int32, (RADII, 128), 1), DEG), 4)
 
     inv_rows = jnp.broadcast_to(inv, (OWN_R, OWN_R)).T
-    for n in range(NQ):
-        wig_p[n] = (wig_p[n].astype(F32) * inv_rows).astype(BF16)
 
     def project(i):
         g = lax.rem(q + i, NQ)
-        w = wig_p[g]
-        both = jnp.concatenate([w, w], axis=0)
-        left = [
-            ordt[pl.ds(h * (ORD // 4) + g * 2, 2)].reshape(BLK, 2 * OWN_R) for h in range(2)
-        ]
-        return dot(jnp.concatenate(left, axis=0), both)
+        w = wig_p[g].astype(F32) * inv_rows
+        both = jnp.concatenate([jnp.where(low_half, w, 0.0), jnp.where(low_half, 0.0, w)], axis=0)
+        return dot(ordt[pl.ds(g * 2, 2)].reshape(BLK, 2 * OWN_R), both.astype(BF16))
 
     def share(i, out):
         g = lax.rem(q + i, NQ)
         acc = [jnp.zeros((RADII, 128), F32)] * 2
-        for kk in range(8):
+        for kk in range(4):
             acc[kk % 2] = jnp.where(slot == kk, out[kk * RADII:(kk + 1) * RADII, :], acc[kk % 2])
         odd = pltpu.roll(acc[1].reshape(RADII // 8, 8, 128), 4, 1).reshape(RADII, 128)
         harm[g] = (acc[0] + odd).astype(BF16).reshape(NX, 16, 128)
@@ -373,7 +373,7 @@
             pltpu.VMEM((PT, OWN_R, 128), F32),
             pltpu.VMEM((NQ, OWN_R, 128), BF16),
             pltpu.VMEM((OWN_P, OWN_R), BF16),
-            pltpu.VMEM((ORD // 2, 2, RADII, 2 * OWN_R), BF16),
+            pltpu.VMEM((ORD // 4, 2, RADII, 2 * OWN_R), BF16),
             pltpu.VMEM((8, 128), F32),
             pltpu.VMEM((NQ - 1, 8, 128), F32),
             pltpu.VMEM((8, 128), F32),
@@ -386,7 +386,8 @@
             pltpu.VMEM((RING, 1, 128), F32),
             pltpu.VMEM((RING - 1, 1, 128), F32),
         ]
-        + [dma(())] * 16,
+        + [dma(())] * 16
+        + [pltpu.SemaphoreType.REGULAR],
         compiler_params=pltpu.CompilerParams(collective_id=0, has_side_effects=True),
         name="recover",
     )(patterns, mask, model.T, wigner, jnp.asarray(syn), jnp.asarray(fwd))

time: 48 us -> 47.7 us (level)
  no operation moved by 1% of the time
where the time goes in v4:
time: 47.7 us; the launch traced here: 47.6 us
  Pallas kernels  46.3 us (97%)
  local copies, waits for them, and re-layouts  1.24 us (3%)
    pallas_call x1, Pallas kernels, local(): pl.pallas_call(kernel, out_shape=jax.ShapeDtypeStruct((2, 64), F32), in_s...  46.3 us
    unnamed x1, local copies, waits for them, and re-layouts  1.24 us

profile of v4, /device:TPU:1, one launch (start us, length us, event | category | flops | bytes accessed | tf_op | source)
XLA Modules:
  0.0 47.6 jit_solution(7995478229115419409)
XLA Ops:
  0.0 46.3 %recover.1 = f32[2,64]{1,0:T(2,128)} custom-call(bf16[384,4096]{1,0:T(8,128)(2,1)} %pat_hbm.1, s32[384]{0:T(512)} %mask_hbm.1, f32[64,1024]{1,0:T(8,128)} %bitcast.2, bf16[128,1024]{1,0:T(8,128)(2,1)} %wig_hbm.1, bf16[256,768]{1,0:T(8,128)(2,1)} %constant.4.clone.syn_hbm, bf16[2,256,768]{2,1,0:T(8,128)(2,1)} %constant.5.clone.fwd_hbm), custom_call_target="tpu_custom_call" | custom-call | tf_op jit(solution)/shard_map/recover/pallas_call | solution.py:358
  46.4 1.2 %copy.8 = f32[64,2]{0,1:T(2,128)} copy(f32[64,2]{0,1:T(2,128)} %bitcast.3) | data formatting | bytes 1024

commit v5 on v4

--- a/solution.py
+++ b/solution.py
@@ -87,7 +87,7 @@
     pat_hbm, mask_hbm, model_hbm, wig_hbm, syn_hbm, fwd_hbm, out_ref,
     pat, mask, model, wig, syn, fwd,
     pat_t, cyc, logs, score, wig_p, wt, ordt,
-    stat, b1, pair, b2, occ1, c1, harm, e1, zsum, zsend, e2,
+    stat, b1, pair, b2, occ1, c1, harm, e1, zsend, e2,
     pat_sem, mask_sem, model_sem, wig_sem, syn_sem, fwd_sem,
     b1_s, b1_r, b2_s, b2_r, c1_s, c1_r, e1_s, e1_r, e2_s, e2_r, known,
 ):
@@ -98,14 +98,13 @@
     z = zh * NZ + zl
 
     def plane_peer(dx, dq):
-        return (lax.rem(x + dx, NX) * NZ + zl, zh * NQ + lax.rem(q + dq, NQ))
+        return (xs[dx] * NZ + zl, zh * NQ + qs[dq])
 
     def ring_peer(dz):
-        far = lax.rem(z + dz, RING)
-        return (x * NZ + lax.rem(far, NZ), lax.div(far, NZ) * NQ + q)
+        return (x * NZ + zls[dz % NZ], lax.div(zs[dz], NZ) * NQ + q)
 
     def pat_peer(dx, dz):
-        return (lax.rem(x + dx, NX) * NZ + lax.rem(zl + dz, NZ), o_id)
+        return (xs[dx] * NZ + zls[dz], o_id)
 
     pat_peers = [(dx, dz) for dz in far_first(NZ) + [0] for dx in (2, 1, 3, 0) if dx or dz]
 
@@ -136,7 +135,10 @@
         load.start()
 
     barrier = pltpu.get_barrier_semaphore()
-    greet(ring_peer(NZ))
+    greet((p_id, (1 - zh) * NQ + q))
+    xs = [lax.rem(x + d, NX) for d in range(NX)]
+    qs = [lax.rem(q + d, NQ) for d in range(NQ)]
+    zls = [lax.rem(zl + d, NZ) for d in range(NZ)]
     for dx, dz in pat_peers:
         if dx == 0 or dz == 0:
             greet(pat_peer(dx, dz))
@@ -236,14 +238,16 @@
     for j in range(NQ - 1):
         mass = mass + b1[j, PT:2 * PT, :] * jnp.exp(b1[j, 0:PT, :] - peak)
     pair[...] = jnp.concatenate([peak, mass, blank], axis=0)
-    send(pair, b2, b2_s, b2_r, ring_peer(NZ))
+    send(pair, b2, b2_s, b2_r, (p_id, (1 - zh) * NQ + q))
+
+    zs = [lax.rem(z + d, RING) for d in range(RING)]
 
     @pl.loop(0, PIX // 128)
     def _(j):
         span = pl.ds(pl.multiple_of(j * 128, 128), 128)
         pat_t[span, :] = pat[:, span].T
 
-    b2_all = whole(b2, b2_s, b2_r, ring_peer(NZ))
+    b2_all = whole(b2, b2_s, b2_r, (p_id, (1 - zh) * NQ + q))
     b2_all.wait_recv()
     far_peak = b2[0:PT, :]
     top = jnp.maximum(peak, far_peak)
@@ -262,8 +266,14 @@
         send(occ1, c1.at[dx * NZ + dz - 1], c1_s, c1_r, pat_peer(dx, dz))
 
     def compress(i, carry):
-        rows = [pl.ds(pl.multiple_of((4 * i + n) * BLK, BLK), BLK) for n in range(4)]
-        sums = [dot(pat_t[r, :], wt[...]) for r in rows]
+        sums = []
+        for n in range(4):
+            first = n // 2 + 8 * (n % 2)
+            rows = [
+                pat_t[pl.ds(pl.multiple_of((16 * i + first + 2 * m) * ANGLES, ANGLES), ANGLES), :]
+                for m in range(4)
+            ]
+            sums.append(dot(jnp.concatenate(rows, axis=0), wt[...]))
         evens = apply_table(fwd[0], sums[0], sums[2])
         odds = apply_table(fwd[1], sums[1], sums[3])
         one, two = (
@@ -291,13 +301,13 @@
     inv_rows = jnp.broadcast_to(inv, (OWN_R, OWN_R)).T
 
     def project(i):
-        g = lax.rem(q + i, NQ)
+        g = qs[i]
         w = wig_p[g].astype(F32) * inv_rows
         both = jnp.concatenate([jnp.where(low_half, w, 0.0), jnp.where(low_half, 0.0, w)], axis=0)
         return dot(ordt[pl.ds(g * 2, 2)].reshape(BLK, 2 * OWN_R), both.astype(BF16))
 
     def share(i, out):
-        g = lax.rem(q + i, NQ)
+        g = qs[i]
         acc = [jnp.zeros((RADII, 128), F32)] * 2
         for kk in range(4):
             acc[kk % 2] = jnp.where(slot == kk, out[kk * RADII:(kk + 1) * RADII, :], acc[kk % 2])
@@ -306,24 +316,21 @@
         for dx in (2, 1, 3, 0):
             if dx or i:
                 send(
-                    harm.at[g, lax.rem(x + dx, NX)], e1.at[dx * NQ + i - 1], e1_s, e1_r,
+                    harm.at[g, xs[dx]], e1.at[dx * NQ + i - 1], e1_s, e1_r,
                     plane_peer(dx, i),
                 )
 
     order = far_first(NQ) + [0]
-    out = project(order[0])
-    for i, later in zip(order, order[1:] + [None]):
-        coming = None if later is None else project(later)
-        share(i, out)
-        out = coming
+    ready = [project(order[0])]
+    for n, i in enumerate(order):
+        ready += [project(later) for later in order[len(ready):n + (3 if n else 2)]]
+        share(i, ready[n])
     e1_all = whole(e1, e1_s, e1_r, plane_peer(1, 0))
     e1_all.wait_recv()
     tot = harm[q, x].astype(F32)
     for j in range(PLANE - 1):
         tot = tot + e1[j].astype(F32)
-    zsum[...] = tot
-    even = zsum[pl.ds(0, 8, stride=2), :]
-    odd = zsum[pl.ds(1, 8, stride=2), :]
+    even, odd = tot[:8], tot[8:]
     first = lane[:8] < 64
     rows = jnp.concatenate(
         [
@@ -335,7 +342,7 @@
     for j in range(RING):
         zsend[j] = rows[j:j + 1, :]
     for j in far_first(RING):
-        send(zsend.at[lax.rem(z + j, RING)], e2.at[j - 1], e2_s, e2_r, ring_peer(j))
+        send(zsend.at[zs[j]], e2.at[j - 1], e2_s, e2_r, ring_peer(j))
     e2_all = whole(e2, e2_s, e2_r, ring_peer(1))
     e2_all.wait_recv()
     fin = zsend[z]
@@ -347,13 +354,17 @@
         copies.wait_send()
     pltpu.make_async_remote_copy(
         src_ref=pair, dst_ref=b2, send_sem=b2_s, recv_sem=b2_r,
-        device_id=ring_peer(NZ), device_id_type=MESH,
+        device_id=(p_id, (1 - zh) * NQ + q), device_id_type=MESH,
     ).wait_send()
 
 
 def local(patterns, mask, model, wigner):
     syn, fwd = tables()
-    hbm = pl.BlockSpec(memory_space=pl.ANY)
+    hbm = pl.BlockSpec(memory_space=pltpu.MemorySpace.HBM)
+
+    def in_hbm(value):
+        return pltpu.with_memory_space_constraint(value, pltpu.MemorySpace.HBM)
+
     dma = pltpu.SemaphoreType.DMA
     out = pl.pallas_call(
         kernel,
@@ -382,15 +393,16 @@
             pltpu.VMEM((NX * NZ - 1, 1, 128), F32),
             pltpu.VMEM((NQ, NX, 16, 128), BF16),
             pltpu.VMEM((PLANE - 1, 16, 128), BF16),
-            pltpu.VMEM((16, 128), F32),
             pltpu.VMEM((RING, 1, 128), F32),
             pltpu.VMEM((RING - 1, 1, 128), F32),
         ]
         + [dma(())] * 16
         + [pltpu.SemaphoreType.REGULAR],
-        compiler_params=pltpu.CompilerParams(collective_id=0, has_side_effects=True),
+        compiler_params=pltpu.CompilerParams(
+            collective_id=0, has_side_effects=True, vmem_limit_bytes=40 * 1024 * 1024
+        ),
         name="recover",
-    )(patterns, mask, model.T, wigner, jnp.asarray(syn), jnp.asarray(fwd))
+    )(*(in_hbm(v) for v in (patterns, mask, model.T, wigner, jnp.asarray(syn), jnp.asarray(fwd))))
     return out.T
 
 

time: 47.7 us -> 46.4 us (0.973)
  local copies, waits for them, and re-layouts: 1.24 us -> 0.56 us
  Pallas kernels: 46.3 us -> 45.8 us
    unnamed x1, local copies, waits for them, and re-layouts: 1.24 us -> 0.56 us
    pallas_call x1, Pallas kernels: 46.3 us -> 45.8 us  [local(): pl.pallas_call(kernel, out_shape=jax.ShapeDtypeStruct((2, 64), F32), in_s...]
where the time goes in v5:
time: 46.4 us; the launch traced here: 46.3 us
  Pallas kernels  45.8 us (99%)
  local copies, waits for them, and re-layouts  0.56 us (1%)
    pallas_call x1, Pallas kernels, local(): pl.pallas_call(kernel, out_shape=jax.ShapeDtypeStruct((2, 64), F32), in_s...  45.8 us

profile of v5, /device:TPU:1, one launch (start us, length us, event | category | flops | bytes accessed | tf_op | source)
XLA Modules:
  0.0 46.3 jit_solution(581370984051980558)
XLA Ops:
  0.0 45.8 %recover.1 = f32[2,64]{1,0:T(2,128)S(1)} custom-call(bf16[384,4096]{1,0:T(8,128)(2,1)} %pat_hbm.1, s32[384]{0:T(512)} %mask_hbm.1, f32[64,1024]{1,0:T(8,128)} %bitcast.3, bf16[128,1024]{1,0:T(8,128)(2,1)} %wig_hbm.1, bf16[256,768]{1,0:T(8,128)(2,1)} %constant.4.clone.syn_hbm, bf16[2,256,768]{2,1,0:T(8,128)(2,1)} %constant.5.clone.fwd_hbm), custom_call_target="tpu_custom_call" | custom-call | tf_op jit(solution)/shard_map/recover/pallas_call | solution.py:369
  45.8 0.6 %copy.8 = f32[64,2]{0,1:T(2,128)} copy(f32[64,2]{0,1:T(2,128)S(1)} %bitcast.2) | data formatting | bytes 1024

commit v6 on v5

--- a/solution.py
+++ b/solution.py
@@ -89,7 +89,7 @@
     pat_t, cyc, logs, score, wig_p, wt, ordt,
     stat, b1, pair, b2, occ1, c1, harm, e1, zsend, e2,
     pat_sem, mask_sem, model_sem, wig_sem, syn_sem, fwd_sem,
-    b1_s, b1_r, b2_s, b2_r, c1_s, c1_r, e1_s, e1_r, e2_s, e2_r, known,
+    b1_s, b1_r, b2_s, b2_r, c1_s, c1_r, e1_s, e1_r, e2_s, e2_r, known, ring_known,
 ):
     p_id = lax.axis_index("pat")
     o_id = lax.axis_index("ori")
@@ -101,7 +101,8 @@
         return (xs[dx] * NZ + zl, zh * NQ + qs[dq])
 
     def ring_peer(dz):
-        return (x * NZ + zls[dz % NZ], lax.div(zs[dz], NZ) * NQ + q)
+        far = lax.rem(z + dz, RING)
+        return (x * NZ + lax.rem(far, NZ), lax.div(far, NZ) * NQ + q)
 
     def pat_peer(dx, dz):
         return (xs[dx] * NZ + zls[dz], o_id)
@@ -135,13 +136,13 @@
         load.start()
 
     barrier = pltpu.get_barrier_semaphore()
-    greet((p_id, (1 - zh) * NQ + q))
+    for d in (4, 12, 3, 13, 2, 14, 1, 15):
+        greet(ring_peer(d))
     xs = [lax.rem(x + d, NX) for d in range(NX)]
     qs = [lax.rem(q + d, NQ) for d in range(NQ)]
     zls = [lax.rem(zl + d, NZ) for d in range(NZ)]
-    for dx, dz in pat_peers:
-        if dx == 0 or dz == 0:
-            greet(pat_peer(dx, dz))
+    for dx in far_first(NX):
+        greet(plane_peer(dx, 0))
     for j in far_first(NQ):
         greet(plane_peer(0, j))
 
@@ -212,13 +213,12 @@
     blank = jnp.zeros((8 - 2 * PT, 128), F32)
     stat[...] = jnp.concatenate(peaks + masses + [blank], axis=0)
 
-    pl.semaphore_wait(barrier, 1 + NX - 1 + NZ - 1 + NQ - 1)
+    pl.semaphore_wait(barrier, 8 + NX - 1 + NQ - 1)
+    for d in (4, 12):
+        pl.semaphore_signal(ring_known, inc=1, device_id=ring_peer(d), device_id_type=MESH)
 
     for j in far_first(NQ):
         send(stat, b1.at[j - 1], b1_s, b1_r, plane_peer(0, j))
-
-    for dx in far_first(NX):
-        pl.semaphore_signal(known, inc=1, device_id=pat_peer(dx, 0), device_id_type=MESH)
 
     fwd_in.wait()
     mask_in.wait()
@@ -238,8 +238,11 @@
     for j in range(NQ - 1):
         mass = mass + b1[j, PT:2 * PT, :] * jnp.exp(b1[j, 0:PT, :] - peak)
     pair[...] = jnp.concatenate([peak, mass, blank], axis=0)
+    pl.semaphore_wait(ring_known, 2)
     send(pair, b2, b2_s, b2_r, (p_id, (1 - zh) * NQ + q))
 
+    for dx in far_first(NX):
+        pl.semaphore_signal(known, inc=1, device_id=plane_peer(dx, 0), device_id_type=MESH)
     zs = [lax.rem(z + d, RING) for d in range(RING)]
 
     @pl.loop(0, PIX // 128)
@@ -397,7 +400,7 @@
             pltpu.VMEM((RING - 1, 1, 128), F32),
         ]
         + [dma(())] * 16
-        + [pltpu.SemaphoreType.REGULAR],
+        + [pltpu.SemaphoreType.REGULAR] * 2,
         compiler_params=pltpu.CompilerParams(
             collective_id=0, has_side_effects=True, vmem_limit_bytes=40 * 1024 * 1024
         ),

time: 46.4 us -> 46 us (level)
  no operation moved by 1% of the time
where the time goes in v6:
time: 46 us; the launch traced here: 45.9 us
  Pallas kernels  45.4 us (99%)
  local copies, waits for them, and re-layouts  0.56 us (1%)
    pallas_call x1, Pallas kernels, local(): pl.pallas_call(kernel, out_shape=jax.ShapeDtypeStruct((2, 64), F32), in_s...  45.4 us

profile of v6, /device:TPU:1, one launch (start us, length us, event | category | flops | bytes accessed | tf_op | source)
XLA Modules:
  0.0 45.9 jit_solution(18305338507206493913)
XLA Ops:
  0.0 45.4 %recover.1 = f32[2,64]{1,0:T(2,128)S(1)} custom-call(bf16[384,4096]{1,0:T(8,128)(2,1)} %pat_hbm.1, s32[384]{0:T(512)} %mask_hbm.1, f32[64,1024]{1,0:T(8,128)} %bitcast.3, bf16[128,1024]{1,0:T(8,128)(2,1)} %wig_hbm.1, bf16[256,768]{1,0:T(8,128)(2,1)} %constant.4.clone.syn_hbm, bf16[2,256,768]{2,1,0:T(8,128)(2,1)} %constant.5.clone.fwd_hbm), custom_call_target="tpu_custom_call" | custom-call | tf_op jit(solution)/shard_map/recover/pallas_call | solution.py:372
  45.4 0.6 %copy.8 = f32[64,2]{0,1:T(2,128)} copy(f32[64,2]{0,1:T(2,128)S(1)} %bitcast.2) | data formatting | bytes 1024

commit v7 on v6

--- a/solution.py
+++ b/solution.py
@@ -180,10 +180,8 @@
         )
         cyc[:, pl.ds(pl.multiple_of(g * 32, 32), 32), :] = out.reshape(NBLK, 32, OWN_R)
 
-    @pl.loop(0, 2)
-    def _(h):
-        for n in range(ORD // 16):
-            gather_cycles(h * (ORD // 16) + n)
+    for g in range(ORD // 8):
+        gather_cycles(g)
 
     syn_in.wait()
 
@@ -199,6 +197,10 @@
 
     total = lax.fori_loop(0, 2, expand, jnp.zeros((8, OWN_R), F32))
     intensity = jnp.sum(total, axis=0, keepdims=True)
+
+    pl.semaphore_wait(barrier, 8 + NX - 1 + NQ - 1)
+    for d in (4, 12):
+        pl.semaphore_signal(ring_known, inc=1, device_id=ring_peer(d), device_id_type=MESH)
 
     pat_in.wait()
     scaled = TEMPER * (dot(pat[...], logs[...]) - intensity)
@@ -212,10 +214,6 @@
         masses.append(jnp.sum(jnp.exp(s - m), axis=0, keepdims=True))
     blank = jnp.zeros((8 - 2 * PT, 128), F32)
     stat[...] = jnp.concatenate(peaks + masses + [blank], axis=0)
-
-    pl.semaphore_wait(barrier, 8 + NX - 1 + NQ - 1)
-    for d in (4, 12):
-        pl.semaphore_signal(ring_known, inc=1, device_id=ring_peer(d), device_id_type=MESH)
 
     for j in far_first(NQ):
         send(stat, b1.at[j - 1], b1_s, b1_r, plane_peer(0, j))

time: 46 us -> 45.7 us (level)
  no operation moved by 1% of the time
where the time goes in v7:
time: 45.7 us; the launch traced here: 45.6 us
  Pallas kernels  45.1 us (99%)
  local copies, waits for them, and re-layouts  0.56 us (1%)
    pallas_call x1, Pallas kernels, local(): pl.pallas_call(kernel, out_shape=jax.ShapeDtypeStruct((2, 64), F32), in_s...  45.1 us

profile of v7, /device:TPU:1, one launch (start us, length us, event | category | flops | bytes accessed | tf_op | source)
XLA Modules:
  0.0 45.6 jit_solution(4611713558400257099)
XLA Ops:
  0.0 45.1 %recover.1 = f32[2,64]{1,0:T(2,128)S(1)} custom-call(bf16[384,4096]{1,0:T(8,128)(2,1)} %pat_hbm.1, s32[384]{0:T(512)} %mask_hbm.1, f32[64,1024]{1,0:T(8,128)} %bitcast.3, bf16[128,1024]{1,0:T(8,128)(2,1)} %wig_hbm.1, bf16[256,768]{1,0:T(8,128)(2,1)} %constant.4.clone.syn_hbm, bf16[2,256,768]{2,1,0:T(8,128)(2,1)} %constant.5.clone.fwd_hbm), custom_call_target="tpu_custom_call" | custom-call | tf_op jit(solution)/shard_map/recover/pallas_call | solution.py:370
  45.1 0.6 %copy.8 = f32[64,2]{0,1:T(2,128)} copy(f32[64,2]{0,1:T(2,128)S(1)} %bitcast.2) | data formatting | bytes 1024

commit v8 on v7

--- a/solution.py
+++ b/solution.py
@@ -107,7 +107,6 @@
     def pat_peer(dx, dz):
         return (xs[dx] * NZ + zls[dz], o_id)
 
-    pat_peers = [(dx, dz) for dz in far_first(NZ) + [0] for dx in (2, 1, 3, 0) if dx or dz]
 
     def greet(peer):
         pl.semaphore_signal(barrier, inc=1, device_id=peer, device_id_type=MESH)
@@ -263,8 +262,14 @@
     occ1[...] = jnp.sum(part, axis=0, keepdims=True)
 
     pl.semaphore_wait(known, NX - 1)
-    for dx, dz in pat_peers:
-        send(occ1, c1.at[dx * NZ + dz - 1], c1_s, c1_r, pat_peer(dx, dz))
+    high_end = lax.div(zl, NZ // 2)
+    for n in range(1, NZ):
+        dz = high_end * n + (1 - high_end) * (NZ - n)
+        for dx in (2, 1, 3, 0):
+            peer = (xs[dx] * NZ + lax.rem(zl + dz, NZ), o_id)
+            send(occ1, c1.at[dx * NZ + dz - 1], c1_s, c1_r, peer)
+    for dx in far_first(NX):
+        send(occ1, c1.at[dx * NZ - 1], c1_s, c1_r, pat_peer(dx, 0))
 
     def compress(i, carry):
         sums = []

time: 45.7 us -> 45.6 us (level)
  no operation moved by 1% of the time
where the time goes in v8:
time: 45.6 us; the launch traced here: 45.5 us
  Pallas kernels  44.9 us (98%)
  local copies, waits for them, and re-layouts  0.56 us (1%)
    pallas_call x1, Pallas kernels, local(): pl.pallas_call(kernel, out_shape=jax.ShapeDtypeStruct((2, 64), F32), in_s...  44.9 us

profile of v8, /device:TPU:1, one launch (start us, length us, event | category | flops | bytes accessed | tf_op | source)
XLA Modules:
  0.0 45.5 jit_solution(14196887682314851405)
XLA Ops:
  0.0 44.9 %recover.1 = f32[2,64]{1,0:T(2,128)S(1)} custom-call(bf16[384,4096]{1,0:T(8,128)(2,1)} %pat_hbm.1, s32[384]{0:T(512)} %mask_hbm.1, f32[64,1024]{1,0:T(8,128)} %bitcast.3, bf16[128,1024]{1,0:T(8,128)(2,1)} %wig_hbm.1, bf16[256,768]{1,0:T(8,128)(2,1)} %constant.4.clone.syn_hbm, bf16[2,256,768]{2,1,0:T(8,128)(2,1)} %constant.5.clone.fwd_hbm), custom_call_target="tpu_custom_call" | custom-call | tf_op jit(solution)/shard_map/recover/pallas_call | solution.py:375
  44.9 0.6 %copy.8 = f32[64,2]{0,1:T(2,128)} copy(f32[64,2]{0,1:T(2,128)S(1)} %bitcast.2) | data formatting | bytes 1024

commit v9 on v8

--- a/solution.py
+++ b/solution.py
@@ -299,7 +299,10 @@
     lax.fori_loop(0, NBLK // 4, compress, 0)
     c1_all = whole(c1, c1_s, c1_r, pat_peer(1, 0))
     c1_all.wait_recv()
-    occ = occ1[...] + jnp.sum(c1[...], axis=0)
+    sums = [occ1[...]] + [c1[j] for j in range(NX * NZ - 1)]
+    while len(sums) > 1:
+        sums = [a + b for a, b in zip(sums[::2], sums[1::2])]
+    occ = sums[0]
     inv = (1.0 / math.sqrt(ORIENTS)) / (occ + 1.0)
 
     slot = lax.rem(lax.div(lax.broadcasted_iota(jnp.int32, (RADII, 128), 1), DEG), 4)
@@ -334,8 +337,10 @@
     e1_all = whole(e1, e1_s, e1_r, plane_peer(1, 0))
     e1_all.wait_recv()
     tot = harm[q, x].astype(F32)
-    for j in range(PLANE - 1):
-        tot = tot + e1[j].astype(F32)
+    sums = [tot] + [e1[j].astype(F32) for j in range(PLANE - 1)]
+    while len(sums) > 1:
+        sums = [a + b for a, b in zip(sums[::2], sums[1::2])]
+    tot = sums[0]
     even, odd = tot[:8], tot[8:]
     first = lane[:8] < 64
     rows = jnp.concatenate(
@@ -352,8 +357,10 @@
     e2_all = whole(e2, e2_s, e2_r, ring_peer(1))
     e2_all.wait_recv()
     fin = zsend[z]
-    for j in range(RING - 1):
-        fin = fin + e2[j]
+    sums = [fin] + [e2[j] for j in range(RING - 1)]
+    while len(sums) > 1:
+        sums = [a + b for a, b in zip(sums[::2], sums[1::2])]
+    fin = sums[0]
     out_ref[0:1, :] = fin[:, :64]
     out_ref[1:2, :] = fin[:, 64:]
     for copies in (b1_all, c1_all, e1_all, e2_all):

time: 45.6 us -> 45.6 us (level)
  no operation moved by 1% of the time
where the time goes in v9:
time: 45.6 us; the launch traced here: 45.4 us
  Pallas kernels  44.9 us (98%)
  local copies, waits for them, and re-layouts  0.56 us (1%)
    pallas_call x1, Pallas kernels, local(): pl.pallas_call(kernel, out_shape=jax.ShapeDtypeStruct((2, 64), F32), in_s...  44.9 us

profile of v9, /device:TPU:1, one launch (start us, length us, event | category | flops | bytes accessed | tf_op | source)
XLA Modules:
  0.0 45.4 jit_solution(269508656892991899)
XLA Ops:
  0.0 44.9 %recover.1 = f32[2,64]{1,0:T(2,128)S(1)} custom-call(bf16[384,4096]{1,0:T(8,128)(2,1)} %pat_hbm.1, s32[384]{0:T(512)} %mask_hbm.1, f32[64,1024]{1,0:T(8,128)} %bitcast.3, bf16[128,1024]{1,0:T(8,128)(2,1)} %wig_hbm.1, bf16[256,768]{1,0:T(8,128)(2,1)} %constant.4.clone.syn_hbm, bf16[2,256,768]{2,1,0:T(8,128)(2,1)} %constant.5.clone.fwd_hbm), custom_call_target="tpu_custom_call" | custom-call | tf_op jit(solution)/shard_map/recover/pallas_call | solution.py:382
  44.9 0.6 %copy.8 = f32[64,2]{0,1:T(2,128)} copy(f32[64,2]{0,1:T(2,128)S(1)} %bitcast.2) | data formatting | bytes 1024

commit v10 on v9

--- a/solution.py
+++ b/solution.py
@@ -332,7 +332,7 @@
     order = far_first(NQ) + [0]
     ready = [project(order[0])]
     for n, i in enumerate(order):
-        ready += [project(later) for later in order[len(ready):n + (3 if n else 2)]]
+        ready += [project(later) for later in order[len(ready):n + (3 if n else 1)]]
         share(i, ready[n])
     e1_all = whole(e1, e1_s, e1_r, plane_peer(1, 0))
     e1_all.wait_recv()

time: 45.6 us -> 45.6 us (level)
  no operation moved by 1% of the time
where the time goes in v10:
time: 45.6 us; the launch traced here: 45.5 us
  Pallas kernels  44.9 us (98%)
  local copies, waits for them, and re-layouts  0.56 us (1%)
    pallas_call x1, Pallas kernels, local(): pl.pallas_call(kernel, out_shape=jax.ShapeDtypeStruct((2, 64), F32), in_s...  44.9 us

profile of v10, /device:TPU:1, one launch (start us, length us, event | category | flops | bytes accessed | tf_op | source)
XLA Modules:
  0.0 45.5 jit_solution(1237338036136905777)
XLA Ops:
  0.0 44.9 %recover.1 = f32[2,64]{1,0:T(2,128)S(1)} custom-call(bf16[384,4096]{1,0:T(8,128)(2,1)} %pat_hbm.1, s32[384]{0:T(512)} %mask_hbm.1, f32[64,1024]{1,0:T(8,128)} %bitcast.3, bf16[128,1024]{1,0:T(8,128)(2,1)} %wig_hbm.1, bf16[256,768]{1,0:T(8,128)(2,1)} %constant.4.clone.syn_hbm, bf16[2,256,768]{2,1,0:T(8,128)(2,1)} %constant.5.clone.fwd_hbm), custom_call_target="tpu_custom_call" | custom-call | tf_op jit(solution)/shard_map/recover/pallas_call | solution.py:382
  45.0 0.6 %copy.8 = f32[64,2]{0,1:T(2,128)} copy(f32[64,2]{0,1:T(2,128)S(1)} %bitcast.2) | data formatting | bytes 1024
